TPU v7x, 32 devices: a whole 2x2x4 slice. The times are simulated.
32 devices in a mesh: gx: 4 (over z), gy: 8 (over y, x, core).
Axes of the slice: x: 2, y: 2, z: 4, core: 2. Of those that a mesh axis runs over, the one named last changes fastest.
Arguments:
- features: bfloat16 [4, 8, 1600, 128], P('gx', 'gy'), may hold values from -6 to 6
- cotangent: bfloat16 [4, 8, 1600, 128], P('gx', 'gy'), may hold values from -6 to 6
- w_order0: bfloat16 [320, 320], replicated, may hold values from -0.3125 to 0.3125
- w_order1: bfloat16 [2, 256, 256], replicated, may hold values from -0.375 to 0.375
- w_order2: bfloat16 [2, 192, 192], replicated, may hold values from -0.4375 to 0.4375
- w_order3: bfloat16 [2, 128, 128], replicated, may hold values from -0.5 to 0.5
- w_order4: bfloat16 [2, 64, 64], replicated, may hold values from -0.75 to 0.75
- to_grid: float32 [100, 25], replicated, may hold values from -1.25 to 1.25
- from_grid: float32 [25, 100], replicated, may hold values from -0.625 to 0.625
- edge_harmonics: float32 [4, 8, 25, 256], P('gx', 'gy'), may hold values from -5 to 5
- edge_source: int32 [4, 8, 256], P('gx', 'gy'), may hold values from 0 to 383, as said below
- edge_target: int32 [4, 8, 256], P('gx', 'gy'), may hold values from 0 to 128, as said below
- send_list: int32 [4, 8, 8, 32], P('gx', 'gy'), may hold values from 0 to 127, as said below
Outputs:
- layer_out: bfloat16 [4, 8, 1600, 128], P('gx', 'gy')
- feature_grad: float32 [4, 8, 1600, 128], P('gx', 'gy')
Inputs may be any that keep to these rules, and one draw needn't show every extreme that they name: `edge_source`: on each cell the live edges come first and padding follows; the number of live edges of a cell is at least 128, and all 256 slots are live on some cell in every draw. Columns below 128 are owned atoms, column 128 + d * 32 + i is entry i of ghost block d. `edge_target`: the value 128 marks a padded edge slot, exactly those slots after a cell's live edges. `send_list`: the 32 entries of one cell and one direction are distinct.
All inputs are finite; a program needn't handle non-finite values.
Results may differ from a plain program's by a relative error of at most 0.0034.
Values may be sent and summed in bfloat16 or wider, within the bound.
No kernel may reach another device: no remote copies, remote signals or barrier semaphores. Data moves between devices by JAX's collectives and lax.ppermute only.
A program may use at most 64 MiB of HBM per device.

v0:
```python
import jax
import jax.numpy as jnp
from jax import lax
from jax.experimental import pallas as pl
from jax.experimental.pallas import tpu as pltpu
from jax.sharding import PartitionSpec as P


F32, BF16, I32 = jnp.float32, jnp.bfloat16, jnp.int32
COEFS = 25
DEGREES = 5
edge_norm = 0.35
SWAPS = ((1, 1), (1, 0), (1, None), (0, 1), (0, 0), (0, None), (None, 1), (None, 0))


def step_of(axis, parity):
    if parity is None:
        return 0
    return jnp.where(lax.rem(lax.axis_index(axis), 2) == parity, 1, -1)


def received_direction(swap):
    place = 3 * (step_of("gx", swap[0]) + 1) + step_of("gy", swap[1]) + 1
    return place - jnp.where(place > 4, 1, 0)


def traded(value, swap):
    nx, ny = lax.axis_size("gx"), lax.axis_size("gy")

    def partner(place, size, parity):
        if parity is None:
            return place
        return (place + (1 if place % 2 == parity else -1)) % size

    pairs = [
        (x * ny + y, partner(x, nx, swap[0]) * ny + partner(y, ny, swap[1]))
        for x in range(nx)
        for y in range(ny)
    ]
    return lax.ppermute(value, ("gx", "gy"), pairs)


def iota(shape, axis):
    return lax.broadcasted_iota(I32, shape, axis)


def dot(a, b):
    return jnp.dot(a, b, preferred_element_type=F32)


def dot_nt(a, b):
    return lax.dot_general(a, b, (((1,), (1,)), ((), ())), preferred_element_type=F32)


def split(value):
    high = value.astype(BF16)
    return high, (value - high.astype(F32)).astype(BF16)


def rows_of(value, part):
    rows, width = value.shape
    quarter = rows // COEFS // 4
    return value.reshape(COEFS, 4, quarter, width)[:, part].reshape(COEFS * quarter, width)


def merged(blocks, part):
    width = blocks[0].shape[1] // 4
    lane = iota((1, 4 * width), 1)
    result = blocks[(3 - part) % 4]
    for m in (2, 1, 0):
        result = jnp.where(lane < (m + 1) * width, blocks[(m - part) % 4], result)
    return result


def lent_lists(lists, atoms):
    place = iota((8, 8), 0)
    wanted = jnp.zeros((8, 8), I32)
    for s, swap in enumerate(SWAPS):
        wanted = jnp.where(place == s, 7 - received_direction(swap), wanted)
    order = (wanted == iota((8, 8), 1)).astype(BF16)
    ghost = lists.shape[1]
    spread = (lax.rem(iota((ghost, atoms), 1), ghost) == iota((ghost, atoms), 0)).astype(BF16)
    chosen = dot(order, lists.astype(F32).astype(BF16)).astype(BF16)
    return dot(chosen, spread).astype(I32)


def lent_pick(lists, q):
    atoms = lists.shape[1]
    row = jnp.concatenate(
        [merged([lists[4 * g + k : 4 * g + k + 1] for k in range(4)], q) for g in range(2)], axis=1
    )
    return (iota((atoms, 2 * atoms), 0) == row).astype(BF16)


def fetch(sources, targets, sems):
    copies = [pltpu.make_async_copy(a, b, sems.at[n]) for n, (a, b) in enumerate(zip(sources, targets))]
    for copy in copies:
        copy.start()
    return copies


def pack_kernel(own_hbm, lists_hbm, *refs):
    outs, own_ref, lists_ref, scratch, sems = refs[:8], refs[8], refs[9], refs[10], refs[11]
    atoms = own_ref.shape[1]
    copies = fetch((lists_hbm, own_hbm), (lists_ref, own_ref), sems)
    copies[0].wait()
    lists = lent_lists(lists_ref[...], atoms)
    picks = [lent_pick(lists, q) for q in range(4)]
    copies[1].wait()
    own = own_ref[...]
    for q in range(4):
        scratch[q] = dot(rows_of(own, q), picks[q])
    for g in range(2):
        for k in range(4):
            parts = [scratch[q, :, atoms * g : atoms * g + atoms] for q in range(4)]
            outs[4 * g + k][...] = merged(parts, k).astype(BF16)


def equal_bits(shape, axis_shift, other_shift):
    return (
        lax.shift_right_logical(iota(shape, 0), axis_shift)
        == lax.shift_right_logical(iota(shape, 1), other_shift)
    ).astype(BF16)


def up_matrices(parts, s):
    points = parts[0].shape[1]
    rows = equal_bits((2 * points, points), 1, 0)
    cols = equal_bits((COEFS, 8 * COEFS), 0, 3)
    wide = [dot(dot_nt(rows, part).astype(BF16), cols) for part in parts]
    row, col = iota(wide[0].shape, 0), iota(wide[0].shape, 1)
    term = lax.bitwise_and(lax.shift_right_logical(col, 1) - s, 3)
    value = jnp.where(term < 2, wide[0], jnp.where(term == 2, wide[1], 0.0))
    return jnp.where(lax.bitwise_and(row, 1) == lax.bitwise_and(col, 1), value, 0.0).astype(BF16)


def down_matrix(part, padded):
    points = part.shape[1]
    shape = (8 * COEFS, 4 * padded)
    row, col = iota(shape, 0), iota(shape, 1)
    slot = sum((col >= m * padded).astype(I32) for m in (1, 2, 3))
    place = iota((points, 4 * padded), 1)
    place = place - padded * sum((place >= m * padded).astype(I32) for m in (1, 2, 3))
    cols = (lax.shift_right_logical(place, 1) == iota((points, 4 * padded), 0)).astype(BF16)
    wide = dot(dot(equal_bits((8 * COEFS, COEFS), 3, 0), part).astype(BF16), cols)
    inner = lax.bitwise_and(col - padded * slot, 1)
    return jnp.where(lax.bitwise_and(row, 7) == 2 * slot + inner, wide, 0.0).astype(BF16)


def channel_pair(value, p):
    width = value.shape[1]
    shaped = value.reshape(COEFS, value.shape[0] // COEFS // 8, 8, width)
    return jnp.concatenate([shaped[:, 2 * p + h] for h in range(2)], axis=2)


def slotted(high, low):
    slot = lax.shift_right_logical(iota((1, 8, 1), 1), 1)
    low = pltpu.roll(low, 2, 1)
    again = pltpu.roll(high, 4, 1)
    width = high.shape[2]
    for s in range(4):
        value = jnp.where(slot == s, high, jnp.where(slot == (s + 1) % 4, low, again))
        yield value.reshape(COEFS * 8, width).astype(BF16)


def filter_rows(columns, harm, filt, q):
    quarter = filt.shape[1] // 4
    scaled = columns.reshape(COEFS, quarter, columns.shape[1]) * harm
    filt[:, q * quarter : (q + 1) * quarter] = scaled.astype(BF16)


def local_kernel(own_ref, *refs):
    given, refs = refs[:11], refs[11:]
    feat_ref, prod_ref, gate_ref, up_ref, down_ref, fdown_ref, part_ref, picks_ref, both_ref = refs[:9]
    turned, kept, refs = refs[9:14], refs[14:23], refs[23:]
    to_ref, from_ref, fup, filt, sems = refs
    copies = fetch(given, (to_ref, from_ref, *kept), sems)
    cot_ref, weights, harm_ref, src_ref, tgt_ref = kept[0], kept[1:6], kept[6], kept[7], kept[8]
    rows, atoms = own_ref.shape
    points = to_ref.shape[1]
    pairs = feat_ref.shape[0]
    padded = feat_ref.shape[1] // 4
    copies[0].wait()
    copies[1].wait()
    to_parts, from_parts = split(to_ref[...]), split(from_ref[...])
    for s in range(4):
        up_ref[s] = up_matrices(to_parts, s)
        fup[s] = up_matrices(from_parts, s)
    for n in range(2):
        down_ref[n] = down_matrix(to_parts[n], padded)
        fdown_ref[n] = down_matrix(from_parts[n], padded)
    for copy in copies[2:]:
        copy.wait()
    own = own_ref[...].astype(F32)
    cot = cot_ref[...].astype(F32)
    for p in range(pairs):
        x = channel_pair(own, p)
        y = channel_pair(cot, p)
        for s, (a, b) in enumerate(zip(slotted(x, jnp.zeros_like(x)), slotted(y, jnp.zeros_like(y)))):
            here = slice(s * padded, s * padded + 2 * points)
            rest = slice(s * padded + 2 * points, (s + 1) * padded)
            feat = dot(up_ref[s], a)
            prod = dot(fup[s], b)
            feat_ref[p, here] = feat
            prod_ref[p, here] = prod
            gate_ref[p, here] = feat * prod
            for ref in (feat_ref, prod_ref):
                ref[p, rest] = jnp.zeros((padded - 2 * points, 2 * atoms), F32)
    src, tgt = src_ref[...], tgt_ref[...]
    edges = src.shape[1]
    ghost = atoms // 4
    target_pick = (iota((atoms, edges), 0) == tgt).astype(BF16)
    both_ref[:atoms] = target_pick
    both_ref[atoms:] = target_pick
    slabs = []
    for swap in SWAPS:
        base = atoms + ghost * received_direction(swap)
        slabs.append((iota((ghost, edges), 0) + base == src).astype(BF16))
    for q in range(4):
        picks_ref[q] = jnp.concatenate(
            [slabs[4 * g + (m - q) % 4] for g in range(2) for m in range(4)], axis=0
        )
    own_pick = (iota((atoms, edges), 0) == src).astype(BF16)
    for q in range(4):
        filter_rows(dot(rows_of(own_ref[...], q), own_pick), harm_ref[...], filt, q)
    part_ref[...] = dot_nt(filt[...].reshape(rows, edges), target_pick)
    turned[0][...] = weights[0][...].T
    for a, b in zip(turned[1:], weights[1:]):
        for n in range(2):
            a[n] = b[n].T


def order_spans(channels):
    spans = []
    offset = DEGREES * channels
    for gap in range(1, DEGREES):
        length = (DEGREES - gap) * channels
        spans.append((offset, offset + length, offset + 2 * length))
        offset += 2 * length
    return spans


def folded(value):
    half = value.shape[1] // 2
    return value[:, :half] + value[:, half:]


def edge_kernel(*refs):
    ghosts, refs = refs[:8], refs[8:]
    weights, turned, refs = refs[:5], refs[5:10], refs[10:]
    picks_ref, both_ref, part_ref, harm_ref, gate_ref, up_ref, down_ref = refs[:7]
    outs, refs = refs[7:15], refs[15:]
    act_ref, dsrc_ref, filt, mixed, agg, dhigh, dlow, dagg, packed = refs
    rows, atoms = part_ref.shape
    channels = rows // COEFS
    edges = both_ref.shape[1]
    pairs = act_ref.shape[0]
    padded = act_ref.shape[1] // 4
    used = up_ref.shape[1]
    blocks = [ghosts[s][...] for s in range(8)]
    for q in range(4):
        taken = jnp.concatenate([merged(blocks[4 * g : 4 * g + 4], q) for g in range(2)], axis=1)
        filter_rows(dot(taken, picks_ref[q]), harm_ref[...], filt, q)
    summed = part_ref[...] + dot_nt(filt[...].reshape(rows, edges), both_ref[:atoms])
    high, low = split(summed)
    mixed[:, :atoms] = high
    mixed[:, atoms:] = low
    zero_rows = DEGREES * channels
    half = 0.5 * edge_norm
    agg[:zero_rows] = folded(dot(weights[0][...], mixed[:zero_rows])) * half
    for w, (begin, mid, end) in zip(weights[1:], order_spans(channels)):
        plus, minus = mixed[begin:mid], mixed[mid:end]
        agg[begin:mid] = folded(dot(w[0], plus) - dot(w[1], minus)) * half
        agg[mid:end] = folded(dot(w[1], plus) + dot(w[0], minus)) * half
    empty = jnp.zeros((padded - used, 2 * atoms), F32)
    for s in range(4):
        rest = slice(s * padded + used, (s + 1) * padded)
        dhigh[rest] = empty.astype(BF16)
        dlow[rest] = empty.astype(BF16)
    for p in range(pairs):
        x = channel_pair(agg[...], p)
        high = x.astype(BF16).astype(F32)
        for s, side in enumerate(slotted(high, x - high)):
            here = slice(s * padded, s * padded + used)
            h = dot(up_ref[s], side)
            t = jnp.tanh(h)
            u = 1.0 + t
            act_ref[p, here] = h * u
            act_ref[p, s * padded + used : (s + 1) * padded] = empty
            a, b = split(gate_ref[p, here] * (u * (1.0 + h * (1.0 - t))))
            dhigh[here] = a
            dlow[here] = b
        down = (dot(down_ref[0], dhigh[...]) + dot(down_ref[0], dlow[...])) * half
        for n in range(2):
            dagg[:, 2 * p + n] = down[:, n * atoms : (n + 1) * atoms].reshape(COEFS, 8, atoms)
    back = dagg[...].reshape(rows, atoms).astype(BF16)

    def keep(begin, end, value):
        high, low = split(value)
        mixed[begin:end, :atoms] = high
        mixed[begin:end, atoms:] = low

    keep(0, zero_rows, dot(turned[0][...], back[:zero_rows]))
    for w, (begin, mid, end) in zip(turned[1:], order_spans(channels)):
        side = jnp.concatenate([back[begin:mid], back[mid:end]], axis=1)
        first, second = dot(w[0], side), dot(w[1], side)
        keep(begin, mid, first[:, :atoms] + second[:, atoms:])
        keep(mid, end, first[:, atoms:] - second[:, :atoms])
    for q in range(4):
        grads = dot(rows_of(mixed[...], q), both_ref[...])
        shaped = grads.reshape(COEFS, grads.shape[0] // COEFS, edges) * harm_ref[...]
        scaled = shaped.reshape(grads.shape).astype(BF16)
        dsrc_ref[q] = scaled
        packed[q] = dot_nt(scaled, picks_ref[q])
    for g in range(2):
        for k in range(4):
            parts = [packed[q, :, atoms * g : atoms * g + atoms] for q in range(4)]
            outs[4 * g + k][...] = merged(parts, k).astype(BF16)


def after_kernel(own_ref, cot_ref, src_ref, down_ref, fdown_ref, act_ref, feat_ref, prod_ref, dsrc_ref, out_ref, grad_ref):
    rows, atoms = own_ref.shape
    channels = rows // COEFS
    edges = src_ref.shape[1]
    own_pick = (iota((atoms, edges), 0) == src_ref[...]).astype(BF16)
    own = own_ref[...].astype(F32).reshape(COEFS, channels // 8, 8, atoms)
    cot = cot_ref[...].astype(F32).reshape(COEFS, channels // 8, 8, atoms)

    def down(parts, value):
        high, low = split(value)
        return dot(parts[0], high) + dot(parts[0], low) + dot(parts[1], high)

    for p in range(channels // 16):
        act = act_ref[p]
        update = down(fdown_ref, act * feat_ref[p])
        grad = down(down_ref, prod_ref[p] * act)
        here = dot_nt(dsrc_ref[p], own_pick).reshape(COEFS, 2, 8, atoms)
        outs = []
        for h in range(2):
            lanes = slice(h * atoms, (h + 1) * atoms)
            outs.append(own[:, 2 * p + h] + update[:, lanes].reshape(COEFS, 8, atoms))
            grad_ref[:, 2 * p + h] = (
                cot[:, 2 * p + h] + grad[:, lanes].reshape(COEFS, 8, atoms) + here[:, h]
            )
        out_ref[:, p] = jnp.concatenate(outs, axis=1).astype(BF16)


def final_kernel(*refs):
    blocks = [r[...] for r in refs[:8]]
    lists_ref, grad_ref, out_hbm, total, sems = refs[8:]
    atoms = grad_ref.shape[2]
    lists = lent_lists(lists_ref[...], atoms)
    copies = []
    for q in range(4):
        taken = jnp.concatenate([merged(blocks[4 * g : 4 * g + 4], q) for g in range(2)], axis=1)
        added = dot_nt(taken, lent_pick(lists, q))
        quarter = added.shape[0] // COEFS
        here = slice(q * quarter, (q + 1) * quarter)
        total[:, here] = grad_ref[:, here] + added.reshape(COEFS, quarter, atoms)
        copies.append(pltpu.make_async_copy(total.at[:, here], out_hbm.at[:, here], sems.at[q]))
        copies[-1].start()
    for copy in copies:
        copy.wait()


VM = pl.BlockSpec(memory_space=pltpu.VMEM)
HB = pl.BlockSpec(memory_space=pltpu.HBM)


def call(kernel, outs, scratch=(), far=(), out_spec=VM):
    def run(*args):
        args = [pltpu.with_memory_space_constraint(x, pltpu.HBM) if n in far else x for n, x in enumerate(args)]
        return pl.pallas_call(
            kernel,
            out_shape=outs,
            in_specs=[HB if n in far else VM for n in range(len(args))],
            out_specs=jax.tree.map(lambda _: out_spec, outs),
            scratch_shapes=list(scratch),
            compiler_params=pltpu.CompilerParams(vmem_limit_bytes=20 * 1024 * 1024),
        )(*args)

    return run


def per_device(
    features,
    cotangent,
    w_order0,
    w_order1,
    w_order2,
    w_order3,
    w_order4,
    to_grid,
    from_grid,
    edge_harmonics,
    edge_source,
    edge_target,
    send_list,
):
    rows, atoms = features.shape[2:]
    channels = rows // COEFS
    edges = edge_source.shape[2]
    points = to_grid.shape[0]
    padded = -(-2 * points // 16) * 16
    pairs = channels // 16
    like = jax.ShapeDtypeStruct
    same = lambda x: like(x.shape, x.dtype)
    block = like((rows // 4, atoms), BF16)
    grid = like((pairs, 4 * padded, 2 * atoms), F32)
    *packed, own, lists = call(
        pack_kernel,
        [block] * 8 + [like((rows, atoms), BF16), like(send_list.shape[2:], I32)],
        [pltpu.VMEM((4, rows // 4, 2 * atoms), F32), pltpu.SemaphoreType.DMA((2,))],
        (0, 1),
    )(features[0, 0], send_list[0, 0])
    ghosts = [traded(packed[s], swap) for s, swap in enumerate(SWAPS)]
    weights = (w_order0, w_order1, w_order2, w_order3, w_order4)
    kept = (
        cotangent[0, 0],
        *weights,
        edge_harmonics[0, 0][:, None, :],
        edge_source[0],
        edge_target[0],
    )
    given = (to_grid.T, from_grid, *kept)
    downs = like((2, 8 * COEFS, 4 * padded), BF16)
    feat, prod, gate, up, down, fdown, part, picks, both, *near = call(
        local_kernel,
        [
            grid,
            grid,
            grid,
            like((4, 2 * points, 8 * COEFS), BF16),
            downs,
            downs,
            like((rows, atoms), F32),
            like((4, 2 * atoms, edges), BF16),
            like((2 * atoms, edges), BF16),
            *map(same, weights),
            *map(same, kept),
        ],
        [
            pltpu.VMEM((COEFS, points), F32),
            pltpu.VMEM((COEFS, points), F32),
            pltpu.VMEM((4, 2 * points, 8 * COEFS), BF16),
            pltpu.VMEM((COEFS, channels, edges), BF16),
            pltpu.SemaphoreType.DMA((len(given),)),
        ],
        range(1, 1 + len(given)),
    )(own, *given)
    turned, (cot, *direct, harm, src, tgt) = near[:5], near[5:]
    *returns, act, dsrc = call(
        edge_kernel,
        [block] * 8 + [grid, like((4, rows // 4, edges), BF16)],
        [
            pltpu.VMEM((COEFS, channels, edges), BF16),
            pltpu.VMEM((rows, 2 * atoms), BF16),
            pltpu.VMEM((rows, atoms), F32),
            pltpu.VMEM((4 * padded, 2 * atoms), BF16),
            pltpu.VMEM((4 * padded, 2 * atoms), BF16),
            pltpu.VMEM((COEFS, channels // 8, 8, atoms), F32),
            pltpu.VMEM((4, rows // 4, 2 * atoms), F32),
        ],
    )(*ghosts, *direct, *turned, picks, both, part, harm, gate, up, down)
    arrived = [traded(returns[s], swap) for s, swap in enumerate(SWAPS)]
    layer, grad = call(
        after_kernel,
        [like((COEFS, pairs, 16, atoms), BF16), like((COEFS, channels // 8, 8, atoms), F32)],
    )(own, cot, src, down, fdown, act, feat, prod, dsrc)
    total = call(
        final_kernel,
        pltpu.HBM((COEFS, channels, atoms), F32),
        [pltpu.VMEM((COEFS, channels, atoms), F32), pltpu.SemaphoreType.DMA((4,))],
        out_spec=HB,
    )(*arrived, lists, grad.reshape(COEFS, channels, atoms))
    return layer.reshape(1, 1, rows, atoms), total.reshape(1, 1, rows, atoms)


def solution(mesh):
    cell = P("gx", "gy", None, None)
    row = P("gx", "gy", None)
    placed = (cell, cell, P(), P(), P(), P(), P(), P(), P(), cell, row, row, cell)
    return jax.shard_map(
        per_device, mesh=mesh, in_specs=placed, out_specs=(cell, cell), check_vma=False
    )
```

profile of v0, /device:TPU:19, one launch (start us, length us, event | category | flops | bytes accessed | tf_op | source)
XLA Modules:
  0.0 52.9 jit_solution(317549275253547021)
XLA Ops:
  0.6 1.8 %shard_map.140 = (bf16[400,128]{1,0:T(8,128)(2,1)S(1)}, bf16[400,128]{1,0:T(8,128)(2,1)S(1)}, bf16[400,128]{1,0:T(8,128)(2,1)S(1)}, bf16[400,128]{1,0:T(8,128)(2...) custom-call(bf16[1600,128]{1,0:T(8,128)(2,1)} %bitcast.12, ...), custom_call_target="tpu_custom_call" | custom-call | tf_op jit(solution)/shard_map/pallas_call | solution.py:373
  2.5 1.7 %collective-permute-start = (bf16[400,128]{1,0:T(8,128)(2,1)S(1)}, bf16[400,128]{1,0:T(8,128)(2,1)S(1)}, u32[]{:S(2)}, u32[]{:S(2)}) collective-permute-start(bf16[400,128]{1,0:T(8,128)(2,1)S(1)} %get-tuple-element.51), channel_id=1, source_target_pairs={{0,31},{1,26},{2,25},{3,28},{4,27},{5,30},{6,29},{7,24},{8,23},{9,... | collective-permute-start | bytes 307208 | tf_op jit(solution)/shard_map/ppermute | solution.py:40
  4.2 0.1 collective-permute-start.1
  4.2 1.2 %collective-permute-start.2 = (bf16[400,128]{1,0:T(8,128)(2,1)S(1)}, bf16[400,128]{1,0:T(8,128)(2,1)S(1)}, u32[]{:S(2)}, u32[]{:S(2)}) collective-permute-start(bf16[400,128]{1,0:T(8,128)(2,1)S(1)} %get-tuple-element.53), channel_id=1, source_target_pairs={{0,24},{1,25},{2,26},{3,27},{4,28},{5,29},{6,30},{7,31},{8,16},{9,... | collective-permute-start | bytes 307208 | tf_op jit(solution)/shard_map/ppermute | solution.py:40
  5.5 4.5 %collective-permute-start.3 = (bf16[400,128]{1,0:T(8,128)(2,1)S(1)}, bf16[400,128]{1,0:T(8,128)(2,1)S(1)}, u32[]{:S(2)}, u32[]{:S(2)}) collective-permute-start(bf16[400,128]{1,0:T(8,128)(2,1)S(1)} %get-tuple-element.54), channel_id=1, source_target_pairs={{0,15},{1,10},{2,9},{3,12},{4,11},{5,14},{6,13},{7,8},{8,7},{9,2},... | collective-permute-start | bytes 307208 | tf_op jit(solution)/shard_map/ppermute | solution.py:40
  10.0 0.0 collective-permute-start.4
  10.0 6.1 %collective-permute-done.refs_0_ = bf16[400,128]{1,0:T(8,128)(2,1)S(1)} collective-permute-done((bf16[400,128]{1,0:T(8,128)(2,1)S(1)}, bf16[400,128]{1,0:T(8,128)(2,1)S(1)}, u32[]{:S(2)}, u32[]{:S(2)}) %collective-permute-start) | collective-permute-done | bytes 102432 | tf_op jit(solution)/shard_map/ppermute | solution.py:40
  16.1 0.0 collective-permute-start.5
  16.1 0.1 collective-permute-done.1.refs_1_
  16.2 2.9 %collective-permute-start.6 = (bf16[400,128]{1,0:T(8,128)(2,1)S(1)}, bf16[400,128]{1,0:T(8,128)(2,1)S(1)}, u32[]{:S(2)}, u32[]{:S(2)}) collective-permute-start(bf16[400,128]{1,0:T(8,128)(2,1)S(1)} %get-tuple-element.57), channel_id=1, source_target_pairs={{0,7},{1,2},{2,1},{3,4},{4,3},{5,6},{6,5},{7,0},{8,15},{9,10},{10,... | collective-permute-start | bytes 307208 | tf_op jit(solution)/shard_map/ppermute | solution.py:40
  19.2 0.0 collective-permute-done.2.refs_2_
  19.2 0.1 collective-permute-start.7
  19.3 4.4 %shard_map.141 = (f32[4,832,256]{2,1,0:T(8,128)S(1)}, f32[4,832,256]{2,1,0:T(8,128)S(1)}, f32[4,832,256]{2,1,0:T(8,128)S(1)}, bf16[4,200,200]{2,1,0:T(8,128)(2,1...) custom-call(bf16[1600,128]{1,0:T(8,128)(2,1)S(1)} %get-tuple-element, ...), custom_call_target="tpu_custom_call" | custom-call | tf_op jit(solution)/shard_map/pallas_call | solution.py:373
  23.8 0.0 collective-permute-done.3.refs_3_
  23.8 0.0 collective-permute-done.4.refs_4_
  23.8 0.0 collective-permute-done.5.refs_5_
  23.8 0.0 collective-permute-done.6.refs_6_
  23.8 0.0 collective-permute-done.7.refs_7_
  23.8 4.8 %shard_map.142 = (bf16[400,128]{1,0:T(8,128)(2,1)S(1)}, bf16[400,128]{1,0:T(8,128)(2,1)S(1)}, bf16[400,128]{1,0:T(8,128)(2,1)S(1)}, bf16[400,128]{1,0:T(8,128)(2...) custom-call(bf16[400,128]{1,0:T(8,128)(2,1)S(1)} %collective-permute, ...), custom_call_target="tpu_custom_call" | custom-call | tf_op jit(solution)/shard_map/pallas_call | solution.py:373
  28.7 2.1 %collective-permute-start.8 = (bf16[400,128]{1,0:T(8,128)(2,1)S(1)}, bf16[400,128]{1,0:T(8,128)(2,1)S(1)}, u32[]{:S(2)}, u32[]{:S(2)}) collective-permute-start(bf16[400,128]{1,0:T(8,128)(2,1)S(1)} %get-tuple-element.80), channel_id=1, source_target_pairs={{0,31},{1,26},{2,25},{3,28},{4,27},{5,30},{6,29},{7,24},{8,23},{9,... | collective-permute-start | bytes 307208 | tf_op jit(solution)/shard_map/ppermute | solution.py:40
  30.8 0.7 %collective-permute-start.9 = (bf16[400,128]{1,0:T(8,128)(2,1)S(1)}, bf16[400,128]{1,0:T(8,128)(2,1)S(1)}, u32[]{:S(2)}, u32[]{:S(2)}) collective-permute-start(bf16[400,128]{1,0:T(8,128)(2,1)S(1)} %get-tuple-element.81), channel_id=1, source_target_pairs={{0,25},{1,24},{2,27},{3,26},{4,29},{5,28},{6,31},{7,30},{8,17},{9,... | collective-permute-start | bytes 307208 | tf_op jit(solution)/shard_map/ppermute | solution.py:40
  31.4 0.6 %collective-permute-start.10 = (bf16[400,128]{1,0:T(8,128)(2,1)S(1)}, bf16[400,128]{1,0:T(8,128)(2,1)S(1)}, u32[]{:S(2)}, u32[]{:S(2)}) collective-permute-start(bf16[400,128]{1,0:T(8,128)(2,1)S(1)} %get-tuple-element.82), channel_id=1, source_target_pairs={{0,24},{1,25},{2,26},{3,27},{4,28},{5,29},{6,30},{7,31},{8,16},{9,... | collective-permute-start | bytes 307208 | tf_op jit(solution)/shard_map/ppermute | solution.py:40
  32.1 2.3 %collective-permute-start.11 = (bf16[400,128]{1,0:T(8,128)(2,1)S(1)}, bf16[400,128]{1,0:T(8,128)(2,1)S(1)}, u32[]{:S(2)}, u32[]{:S(2)}) collective-permute-start(bf16[400,128]{1,0:T(8,128)(2,1)S(1)} %get-tuple-element.83), channel_id=1, source_target_pairs={{0,15},{1,10},{2,9},{3,12},{4,11},{5,14},{6,13},{7,8},{8,7},{9,2},... | collective-permute-start | bytes 307208 | tf_op jit(solution)/shard_map/ppermute | solution.py:40
  34.4 0.0 collective-permute-start.12
  34.4 8.8 %collective-permute-done.8.refs_0_ = bf16[400,128]{1,0:T(8,128)(2,1)S(1)} collective-permute-done((bf16[400,128]{1,0:T(8,128)(2,1)S(1)}, bf16[400,128]{1,0:T(8,128)(2,1)S(1)}, u32[]{:S(2)}, u32[]{:S(2)}) %collective-permute-start.8) | collective-permute-done | bytes 102432 | tf_op jit(solution)/shard_map/ppermute | solution.py:40
  43.2 0.0 collective-permute-start.13
  43.2 1.5 %collective-permute-done.9.refs_1_ = bf16[400,128]{1,0:T(8,128)(2,1)S(1)} collective-permute-done((bf16[400,128]{1,0:T(8,128)(2,1)S(1)}, bf16[400,128]{1,0:T(8,128)(2,1)S(1)}, u32[]{:S(2)}, u32[]{:S(2)}) %collective-permute-start.9) | collective-permute-done | bytes 102432 | tf_op jit(solution)/shard_map/ppermute | solution.py:40
  44.7 1.0 %collective-permute-start.14 = (bf16[400,128]{1,0:T(8,128)(2,1)S(1)}, bf16[400,128]{1,0:T(8,128)(2,1)S(1)}, u32[]{:S(2)}, u32[]{:S(2)}) collective-permute-start(bf16[400,128]{1,0:T(8,128)(2,1)S(1)} %get-tuple-element.86), channel_id=1, source_target_pairs={{0,7},{1,2},{2,1},{3,4},{4,3},{5,6},{6,5},{7,0},{8,15},{9,10},{10,... | collective-permute-start | bytes 307208 | tf_op jit(solution)/shard_map/ppermute | solution.py:40
  45.6 1.2 %collective-permute-done.10.refs_2_ = bf16[400,128]{1,0:T(8,128)(2,1)S(1)} collective-permute-done((bf16[400,128]{1,0:T(8,128)(2,1)S(1)}, bf16[400,128]{1,0:T(8,128)(2,1)S(1)}, u32[]{:S(2)}, u32[]{:S(2)}) %collective-permute-start.10) | collective-permute-done | bytes 102432 | tf_op jit(solution)/shard_map/ppermute | solution.py:40
  46.9 0.4 collective-permute-start.15
  47.2 4.1 %shard_map.143 = (bf16[25,4,16,128]{3,2,1,0:T(8,128)(2,1)}, f32[25,8,8,128]{3,2,1,0:T(8,128)S(1)}) custom-call(bf16[1600,128]{1,0:T(8,128)(2,1)S(1)} %get-tuple-element.46.own_ref, bf16[1600,128]{1,0:T(8,128)(2,1)S(1)} %get-tuple-element.47.cot_ref, s32[1,256]{1,0:T(1,128)S(1)} %get-tuple-element.48.src_ref, ...), custom_call_target="tpu_custom_call" | custom-call | tf_op jit(solution)/shard_map/pallas_call | solution.py:373
  51.4 0.0 collective-permute-done.11.refs_3_
  51.4 0.0 collective-permute-done.12.refs_4_
  51.4 0.0 collective-permute-done.13.refs_5_
  51.4 0.0 collective-permute-done.14.refs_6_
  51.4 0.0 collective-permute-done.15.refs_7_
  51.4 1.5 %shard_map.144 = f32[25,64,128]{2,1,0:T(8,128)} custom-call(bf16[400,128]{1,0:T(8,128)(2,1)S(1)} %collective-permute-done.8.refs_0_, bf16[400,128]{1,0:T(8,128)(2,1)S(1)} %collective-permute-done.9.refs_1_, bf16[400,128]{1,0:T(8,128)(2,1)S(1)} %collective-permute-done.10.refs_2_, bf16[400,128]{1,0:T(8,128)(2,1)S(1)} %collective-permute-done.11.refs_3_, ...), custom_call_target="tpu_custom_call" | custom-call | tf_op jit(solution)/shard_map/pallas_call | solution.py:373
Async XLA Ops:
  2.5 13.6 %collective-permute-start = (bf16[400,128]{1,0:T(8,128)(2,1)S(1)}, bf16[400,128]{1,0:T(8,128)(2,1)S(1)}, u32[]{:S(2)}, u32[]{:S(2)}) collective-permute-start(bf16[400,128]{1,0:T(8,128)(2,1)S(1)} %get-tuple-element.51), channel_id=1, source_target_pairs={{0,31},{1,26},{2,25},{3,28},{4,27},{5,30},{6,29},{7,24},{8,23},{9,... | collective-permute-start | bytes 307208 | tf_op jit(solution)/shard_map/ppermute | solution.py:40
  4.2 12.1 %collective-permute-start.1 = (bf16[400,128]{1,0:T(8,128)(2,1)S(1)}, bf16[400,128]{1,0:T(8,128)(2,1)S(1)}, u32[]{:S(2)}, u32[]{:S(2)}) collective-permute-start(bf16[400,128]{1,0:T(8,128)(2,1)S(1)} %get-tuple-element.52), channel_id=1, source_target_pairs={{0,25},{1,24},{2,27},{3,26},{4,29},{5,28},{6,31},{7,30},{8,17},{9,... | collective-permute-start | bytes 307208 | tf_op jit(solution)/shard_map/ppermute | solution.py:40
  4.2 14.9 %collective-permute-start.2 = (bf16[400,128]{1,0:T(8,128)(2,1)S(1)}, bf16[400,128]{1,0:T(8,128)(2,1)S(1)}, u32[]{:S(2)}, u32[]{:S(2)}) collective-permute-start(bf16[400,128]{1,0:T(8,128)(2,1)S(1)} %get-tuple-element.53), channel_id=1, source_target_pairs={{0,24},{1,25},{2,26},{3,27},{4,28},{5,29},{6,30},{7,31},{8,16},{9,... | collective-permute-start | bytes 307208 | tf_op jit(solution)/shard_map/ppermute | solution.py:40
  5.5 18.3 %collective-permute-start.3 = (bf16[400,128]{1,0:T(8,128)(2,1)S(1)}, bf16[400,128]{1,0:T(8,128)(2,1)S(1)}, u32[]{:S(2)}, u32[]{:S(2)}) collective-permute-start(bf16[400,128]{1,0:T(8,128)(2,1)S(1)} %get-tuple-element.54), channel_id=1, source_target_pairs={{0,15},{1,10},{2,9},{3,12},{4,11},{5,14},{6,13},{7,8},{8,7},{9,2},... | collective-permute-start | bytes 307208 | tf_op jit(solution)/shard_map/ppermute | solution.py:40
  10.0 13.8 %collective-permute-start.4 = (bf16[400,128]{1,0:T(8,128)(2,1)S(1)}, bf16[400,128]{1,0:T(8,128)(2,1)S(1)}, u32[]{:S(2)}, u32[]{:S(2)}) collective-permute-start(bf16[400,128]{1,0:T(8,128)(2,1)S(1)} %get-tuple-element.55), channel_id=1, source_target_pairs={{0,9},{1,8},{2,11},{3,10},{4,13},{5,12},{6,15},{7,14},{8,1},{9,0},... | collective-permute-start | bytes 307208 | tf_op jit(solution)/shard_map/ppermute | solution.py:40
  16.1 7.7 %collective-permute-start.5 = (bf16[400,128]{1,0:T(8,128)(2,1)S(1)}, bf16[400,128]{1,0:T(8,128)(2,1)S(1)}, u32[]{:S(2)}, u32[]{:S(2)}) collective-permute-start(bf16[400,128]{1,0:T(8,128)(2,1)S(1)} %get-tuple-element.56), channel_id=1, source_target_pairs={{0,8},{1,9},{2,10},{3,11},{4,12},{5,13},{6,14},{7,15},{8,0},{9,1},... | collective-permute-start | bytes 307208 | tf_op jit(solution)/shard_map/ppermute | solution.py:40
  16.2 7.6 %collective-permute-start.6 = (bf16[400,128]{1,0:T(8,128)(2,1)S(1)}, bf16[400,128]{1,0:T(8,128)(2,1)S(1)}, u32[]{:S(2)}, u32[]{:S(2)}) collective-permute-start(bf16[400,128]{1,0:T(8,128)(2,1)S(1)} %get-tuple-element.57), channel_id=1, source_target_pairs={{0,7},{1,2},{2,1},{3,4},{4,3},{5,6},{6,5},{7,0},{8,15},{9,10},{10,... | collective-permute-start | bytes 307208 | tf_op jit(solution)/shard_map/ppermute | solution.py:40
  19.2 4.6 %collective-permute-start.7 = (bf16[400,128]{1,0:T(8,128)(2,1)S(1)}, bf16[400,128]{1,0:T(8,128)(2,1)S(1)}, u32[]{:S(2)}, u32[]{:S(2)}) collective-permute-start(bf16[400,128]{1,0:T(8,128)(2,1)S(1)} %get-tuple-element.58), channel_id=1, source_target_pairs={{0,1},{1,0},{2,3},{3,2},{4,5},{5,4},{6,7},{7,6},{8,9},{9,8},{10,11... | collective-permute-start | bytes 307208 | tf_op jit(solution)/shard_map/ppermute | solution.py:40
  28.7 14.5 %collective-permute-start.8 = (bf16[400,128]{1,0:T(8,128)(2,1)S(1)}, bf16[400,128]{1,0:T(8,128)(2,1)S(1)}, u32[]{:S(2)}, u32[]{:S(2)}) collective-permute-start(bf16[400,128]{1,0:T(8,128)(2,1)S(1)} %get-tuple-element.80), channel_id=1, source_target_pairs={{0,31},{1,26},{2,25},{3,28},{4,27},{5,30},{6,29},{7,24},{8,23},{9,... | collective-permute-start | bytes 307208 | tf_op jit(solution)/shard_map/ppermute | solution.py:40
  30.8 13.9 %collective-permute-start.9 = (bf16[400,128]{1,0:T(8,128)(2,1)S(1)}, bf16[400,128]{1,0:T(8,128)(2,1)S(1)}, u32[]{:S(2)}, u32[]{:S(2)}) collective-permute-start(bf16[400,128]{1,0:T(8,128)(2,1)S(1)} %get-tuple-element.81), channel_id=1, source_target_pairs={{0,25},{1,24},{2,27},{3,26},{4,29},{5,28},{6,31},{7,30},{8,17},{9,... | collective-permute-start | bytes 307208 | tf_op jit(solution)/shard_map/ppermute | solution.py:40
  31.4 15.4 %collective-permute-start.10 = (bf16[400,128]{1,0:T(8,128)(2,1)S(1)}, bf16[400,128]{1,0:T(8,128)(2,1)S(1)}, u32[]{:S(2)}, u32[]{:S(2)}) collective-permute-start(bf16[400,128]{1,0:T(8,128)(2,1)S(1)} %get-tuple-element.82), channel_id=1, source_target_pairs={{0,24},{1,25},{2,26},{3,27},{4,28},{5,29},{6,30},{7,31},{8,16},{9,... | collective-permute-start | bytes 307208 | tf_op jit(solution)/shard_map/ppermute | solution.py:40
  32.1 19.3 %collective-permute-start.11 = (bf16[400,128]{1,0:T(8,128)(2,1)S(1)}, bf16[400,128]{1,0:T(8,128)(2,1)S(1)}, u32[]{:S(2)}, u32[]{:S(2)}) collective-permute-start(bf16[400,128]{1,0:T(8,128)(2,1)S(1)} %get-tuple-element.83), channel_id=1, source_target_pairs={{0,15},{1,10},{2,9},{3,12},{4,11},{5,14},{6,13},{7,8},{8,7},{9,2},... | collective-permute-start | bytes 307208 | tf_op jit(solution)/shard_map/ppermute | solution.py:40
  34.4 17.0 %collective-permute-start.12 = (bf16[400,128]{1,0:T(8,128)(2,1)S(1)}, bf16[400,128]{1,0:T(8,128)(2,1)S(1)}, u32[]{:S(2)}, u32[]{:S(2)}) collective-permute-start(bf16[400,128]{1,0:T(8,128)(2,1)S(1)} %get-tuple-element.84), channel_id=1, source_target_pairs={{0,9},{1,8},{2,11},{3,10},{4,13},{5,12},{6,15},{7,14},{8,1},{9,0},... | collective-permute-start | bytes 307208 | tf_op jit(solution)/shard_map/ppermute | solution.py:40
  43.2 8.2 %collective-permute-start.13 = (bf16[400,128]{1,0:T(8,128)(2,1)S(1)}, bf16[400,128]{1,0:T(8,128)(2,1)S(1)}, u32[]{:S(2)}, u32[]{:S(2)}) collective-permute-start(bf16[400,128]{1,0:T(8,128)(2,1)S(1)} %get-tuple-element.85), channel_id=1, source_target_pairs={{0,8},{1,9},{2,10},{3,11},{4,12},{5,13},{6,14},{7,15},{8,0},{9,1},... | collective-permute-start | bytes 307208 | tf_op jit(solution)/shard_map/ppermute | solution.py:40
  44.7 6.7 %collective-permute-start.14 = (bf16[400,128]{1,0:T(8,128)(2,1)S(1)}, bf16[400,128]{1,0:T(8,128)(2,1)S(1)}, u32[]{:S(2)}, u32[]{:S(2)}) collective-permute-start(bf16[400,128]{1,0:T(8,128)(2,1)S(1)} %get-tuple-element.86), channel_id=1, source_target_pairs={{0,7},{1,2},{2,1},{3,4},{4,3},{5,6},{6,5},{7,0},{8,15},{9,10},{10,... | collective-permute-start | bytes 307208 | tf_op jit(solution)/shard_map/ppermute | solution.py:40
  46.9 4.6 %collective-permute-start.15 = (bf16[400,128]{1,0:T(8,128)(2,1)S(1)}, bf16[400,128]{1,0:T(8,128)(2,1)S(1)}, u32[]{:S(2)}, u32[]{:S(2)}) collective-permute-start(bf16[400,128]{1,0:T(8,128)(2,1)S(1)} %get-tuple-element.87), channel_id=1, source_target_pairs={{0,1},{1,0},{2,3},{3,2},{4,5},{5,4},{6,7},{7,6},{8,9},{9,8},{10,11... | collective-permute-start | bytes 307208 | tf_op jit(solution)/shard_map/ppermute | solution.py:40
where the time goes:
time: 53.2 us; the launch traced here: 52.9 us
  waiting for transfers between devices  17.8 us (33%)
  starting transfers between devices  17.7 us (33%)
  Pallas kernels  16.8 us (32%)
  between operations  0.72 us (1%)
    ppermute x16, waiting for transfers between devices, traded(): return lax.ppermute(value, ('gx', 'gy'), pairs)  17.8 us
    ppermute x16, starting transfers between devices, traded(): return lax.ppermute(value, ('gx', 'gy'), pairs)  17.7 us
    pallas_call x5, Pallas kernels, run(): pl.pallas_call(kernel, out_shape=outs, in_specs=[HB if n in far else VM f...  16.8 us
  transfers between devices with their start and end apart: 16, of which 5 were waited for; matrix products, arithmetic and copies ran while one was open for 0% of the time, Pallas kernels for 16%

commit v1 on v0

--- a/solution.py
+++ b/solution.py
@@ -10,7 +10,7 @@
 COEFS = 25
 DEGREES = 5
 edge_norm = 0.35
-SWAPS = ((1, 1), (1, 0), (1, None), (0, 1), (0, 0), (0, None), (None, 1), (None, 0))
+SWAPS = ((1, None), (0, None), (1, 1), (0, 1), (1, 0), (0, 0), (None, 1), (None, 0))
 
 
 def step_of(axis, parity):
@@ -84,12 +84,12 @@
     return dot(chosen, spread).astype(I32)
 
 
-def lent_pick(lists, q):
+def lent_pick(lists, q, groups):
     atoms = lists.shape[1]
     row = jnp.concatenate(
-        [merged([lists[4 * g + k : 4 * g + k + 1] for k in range(4)], q) for g in range(2)], axis=1
+        [merged([lists[4 * g + k : 4 * g + k + 1] for k in range(4)], q) for g in groups], axis=1
     )
-    return (iota((atoms, 2 * atoms), 0) == row).astype(BF16)
+    return (iota((atoms, row.shape[1]), 0) == row).astype(BF16)
 
 
 def fetch(sources, targets, sems):
@@ -99,21 +99,25 @@
     return copies
 
 
+def pack_group(own, lists, outs, scratch, g):
+    for q in range(4):
+        scratch[q] = dot(rows_of(own, q), lent_pick(lists, q, (g,)))
+    for k in range(4):
+        outs[k][...] = merged([scratch[q] for q in range(4)], k).astype(BF16)
+
+
 def pack_kernel(own_hbm, lists_hbm, *refs):
-    outs, own_ref, lists_ref, scratch, sems = refs[:8], refs[8], refs[9], refs[10], refs[11]
-    atoms = own_ref.shape[1]
+    outs, own_ref, lists_ref, scratch, sems = refs[:4], refs[4], refs[5], refs[6], refs[7]
     copies = fetch((lists_hbm, own_hbm), (lists_ref, own_ref), sems)
     copies[0].wait()
-    lists = lent_lists(lists_ref[...], atoms)
-    picks = [lent_pick(lists, q) for q in range(4)]
+    lists = lent_lists(lists_ref[...], own_ref.shape[1])
     copies[1].wait()
-    own = own_ref[...]
-    for q in range(4):
-        scratch[q] = dot(rows_of(own, q), picks[q])
-    for g in range(2):
-        for k in range(4):
-            parts = [scratch[q, :, atoms * g : atoms * g + atoms] for q in range(4)]
-            outs[4 * g + k][...] = merged(parts, k).astype(BF16)
+    pack_group(own_ref[...], lists, outs, scratch, 0)
+
+
+def pack_rest_kernel(own_ref, lists_ref, *refs):
+    lists = lent_lists(lists_ref[...], own_ref.shape[1])
+    pack_group(own_ref[...], lists, refs[:4], refs[4], 1)
 
 
 def equal_bits(shape, axis_shift, other_shift):
@@ -154,13 +158,13 @@
 
 
 def slotted(high, low):
-    slot = lax.shift_right_logical(iota((1, 8, 1), 1), 1)
-    low = pltpu.roll(low, 2, 1)
-    again = pltpu.roll(high, 4, 1)
-    width = high.shape[2]
+    shape = (COEFS * 8, high.shape[2])
+    slot = lax.bitwise_and(lax.shift_right_logical(iota((shape[0], 1), 0), 1), 3)
+    low = pltpu.roll(low, 2, 1).reshape(shape).astype(BF16)
+    again = pltpu.roll(high, 4, 1).reshape(shape).astype(BF16)
+    high = high.reshape(shape).astype(BF16)
     for s in range(4):
-        value = jnp.where(slot == s, high, jnp.where(slot == (s + 1) % 4, low, again))
-        yield value.reshape(COEFS * 8, width).astype(BF16)
+        yield jnp.where(slot == s, high, jnp.where(slot == (s + 1) % 4, low, again))
 
 
 def filter_rows(columns, harm, filt, q):
@@ -249,8 +253,8 @@
     ghosts, refs = refs[:8], refs[8:]
     weights, turned, refs = refs[:5], refs[5:10], refs[10:]
     picks_ref, both_ref, part_ref, harm_ref, gate_ref, up_ref, down_ref = refs[:7]
-    outs, refs = refs[7:15], refs[15:]
-    act_ref, dsrc_ref, filt, mixed, agg, dhigh, dlow, dagg, packed = refs
+    outs, refs = refs[7:11], refs[11:]
+    act_ref, dsrc_ref, filt, mixed, agg, dgrid, dagg, packed = refs
     rows, atoms = part_ref.shape
     channels = rows // COEFS
     edges = both_ref.shape[1]
@@ -275,8 +279,7 @@
     empty = jnp.zeros((padded - used, 2 * atoms), F32)
     for s in range(4):
         rest = slice(s * padded + used, (s + 1) * padded)
-        dhigh[rest] = empty.astype(BF16)
-        dlow[rest] = empty.astype(BF16)
+        dgrid[rest] = empty.astype(BF16)
     for p in range(pairs):
         x = channel_pair(agg[...], p)
         high = x.astype(BF16).astype(F32)
@@ -285,12 +288,11 @@
             h = dot(up_ref[s], side)
             t = jnp.tanh(h)
             u = 1.0 + t
-            act_ref[p, here] = h * u
+            act = h * u
+            act_ref[p, here] = act
             act_ref[p, s * padded + used : (s + 1) * padded] = empty
-            a, b = split(gate_ref[p, here] * (u * (1.0 + h * (1.0 - t))))
-            dhigh[here] = a
-            dlow[here] = b
-        down = (dot(down_ref[0], dhigh[...]) + dot(down_ref[0], dlow[...])) * half
+            dgrid[here] = (gate_ref[p, here] * (u + act * (1.0 - t))).astype(BF16)
+        down = dot(down_ref[0], dgrid[...]) * half
         for n in range(2):
             dagg[:, 2 * p + n] = down[:, n * atoms : (n + 1) * atoms].reshape(COEFS, 8, atoms)
     back = dagg[...].reshape(rows, atoms).astype(BF16)
@@ -311,11 +313,19 @@
         shaped = grads.reshape(COEFS, grads.shape[0] // COEFS, edges) * harm_ref[...]
         scaled = shaped.reshape(grads.shape).astype(BF16)
         dsrc_ref[q] = scaled
-        packed[q] = dot_nt(scaled, picks_ref[q])
-    for g in range(2):
-        for k in range(4):
-            parts = [packed[q, :, atoms * g : atoms * g + atoms] for q in range(4)]
-            outs[4 * g + k][...] = merged(parts, k).astype(BF16)
+    return_group(dsrc_ref, picks_ref, outs, packed, 0)
+
+
+def return_group(dsrc_ref, picks_ref, outs, packed, g):
+    half = picks_ref.shape[1] // 2
+    for q in range(4):
+        packed[q] = dot_nt(dsrc_ref[q], picks_ref[q, g * half : (g + 1) * half]).astype(BF16)
+    for k in range(4):
+        outs[k][...] = merged([packed[q] for q in range(4)], k)
+
+
+def edge_rest_kernel(dsrc_ref, picks_ref, *refs):
+    return_group(dsrc_ref, picks_ref, refs[:4], refs[4], 1)
 
 
 def after_kernel(own_ref, cot_ref, src_ref, down_ref, fdown_ref, act_ref, feat_ref, prod_ref, dsrc_ref, out_ref, grad_ref):
@@ -353,7 +363,7 @@
     copies = []
     for q in range(4):
         taken = jnp.concatenate([merged(blocks[4 * g : 4 * g + 4], q) for g in range(2)], axis=1)
-        added = dot_nt(taken, lent_pick(lists, q))
+        added = dot_nt(taken, lent_pick(lists, q, (0, 1)))
         quarter = added.shape[0] // COEFS
         here = slice(q * quarter, (q + 1) * quarter)
         total[:, here] = grad_ref[:, here] + added.reshape(COEFS, quarter, atoms)
@@ -409,10 +419,11 @@
     grid = like((pairs, 4 * padded, 2 * atoms), F32)
     *packed, own, lists = call(
         pack_kernel,
-        [block] * 8 + [like((rows, atoms), BF16), like(send_list.shape[2:], I32)],
-        [pltpu.VMEM((4, rows // 4, 2 * atoms), F32), pltpu.SemaphoreType.DMA((2,))],
+        [block] * 4 + [like((rows, atoms), BF16), like(send_list.shape[2:], I32)],
+        [pltpu.VMEM((4, rows // 4, atoms), F32), pltpu.SemaphoreType.DMA((2,))],
         (0, 1),
     )(features[0, 0], send_list[0, 0])
+    packed += call(pack_rest_kernel, [block] * 4, [pltpu.VMEM((4, rows // 4, atoms), F32)])(own, lists)
     ghosts = [traded(packed[s], swap) for s, swap in enumerate(SWAPS)]
     weights = (w_order0, w_order1, w_order2, w_order3, w_order4)
     kept = (
@@ -451,17 +462,17 @@
     turned, (cot, *direct, harm, src, tgt) = near[:5], near[5:]
     *returns, act, dsrc = call(
         edge_kernel,
-        [block] * 8 + [grid, like((4, rows // 4, edges), BF16)],
+        [block] * 4 + [grid, like((4, rows // 4, edges), BF16)],
         [
             pltpu.VMEM((COEFS, channels, edges), BF16),
             pltpu.VMEM((rows, 2 * atoms), BF16),
             pltpu.VMEM((rows, atoms), F32),
             pltpu.VMEM((4 * padded, 2 * atoms), BF16),
-            pltpu.VMEM((4 * padded, 2 * atoms), BF16),
             pltpu.VMEM((COEFS, channels // 8, 8, atoms), F32),
-            pltpu.VMEM((4, rows // 4, 2 * atoms), F32),
+            pltpu.VMEM((4, rows // 4, atoms), BF16),
         ],
     )(*ghosts, *direct, *turned, picks, both, part, harm, gate, up, down)
+    returns += call(edge_rest_kernel, [block] * 4, [pltpu.VMEM((4, rows // 4, atoms), BF16)])(dsrc, picks)
     arrived = [traded(returns[s], swap) for s, swap in enumerate(SWAPS)]
     layer, grad = call(
         after_kernel,

time: 53.2 us -> 44.2 us (0.83)
  the two profiles are of different devices: /device:TPU:19 before, /device:TPU:0 now
where the time goes in v1:
time: 44.2 us; the launch traced here: 43.9 us
  starting transfers between devices  23.5 us (53%)
  Pallas kernels  15.9 us (36%)
  waiting for transfers between devices  3.77 us (9%)
  between operations  0.72 us (2%)
    ppermute x16, starting transfers between devices, traded(): return lax.ppermute(value, ('gx', 'gy'), pairs)  23.5 us
    pallas_call x7, Pallas kernels, run(): pl.pallas_call(kernel, out_shape=outs, in_specs=[HB if n in far else VM f...  15.9 us
    ppermute x16, waiting for transfers between devices, traded(): return lax.ppermute(value, ('gx', 'gy'), pairs)  3.77 us
  transfers between devices with their start and end apart: 16, of which 5 were waited for; matrix products, arithmetic and copies ran while one was open for 0% of the time, Pallas kernels for 21%

profile of v1, /device:TPU:0, one launch (start us, length us, event | category | flops | bytes accessed | tf_op | source)
XLA Modules:
  0.0 43.9 jit_solution(243360781096933676)
XLA Ops:
  0.6 1.4 %shard_map.140 = (bf16[400,128]{1,0:T(8,128)(2,1)S(1)}, bf16[400,128]{1,0:T(8,128)(2,1)S(1)}, bf16[400,128]{1,0:T(8,128)(2,1)S(1)}, bf16[400,128]{1,0:T(8,128)(2...) custom-call(bf16[1600,128]{1,0:T(8,128)(2,1)} %bitcast.12, s32[8,32]{1,0:T(8,128)} %bitcast.16), custom_call_target="tpu_custom_call" | custom-call | tf_op jit(solution)/shard_map/pallas_call | solution.py:383
  2.0 5.1 %collective-permute-start = (bf16[400,128]{1,0:T(8,128)(2,1)S(1)}, bf16[400,128]{1,0:T(8,128)(2,1)S(1)}, u32[]{:S(2)}, u32[]{:S(2)}) collective-permute-start(bf16[400,128]{1,0:T(8,128)(2,1)S(1)} %get-tuple-element.51), channel_id=1, source_target_pairs={{0,24},{1,25},{2,26},{3,27},{4,28},{5,29},{6,30},{7,31},{8,16},{9,... | collective-permute-start | bytes 307208 | tf_op jit(solution)/shard_map/ppermute | solution.py:40
  7.2 0.0 collective-permute-start.1
  7.2 1.7 %collective-permute-start.2 = (bf16[400,128]{1,0:T(8,128)(2,1)S(1)}, bf16[400,128]{1,0:T(8,128)(2,1)S(1)}, u32[]{:S(2)}, u32[]{:S(2)}) collective-permute-start(bf16[400,128]{1,0:T(8,128)(2,1)S(1)} %get-tuple-element.53), channel_id=1, source_target_pairs={{0,31},{1,26},{2,25},{3,28},{4,27},{5,30},{6,29},{7,24},{8,23},{9,... | collective-permute-start | bytes 307208 | tf_op jit(solution)/shard_map/ppermute | solution.py:40
  8.8 1.1 %collective-permute-start.3 = (bf16[400,128]{1,0:T(8,128)(2,1)S(1)}, bf16[400,128]{1,0:T(8,128)(2,1)S(1)}, u32[]{:S(2)}, u32[]{:S(2)}) collective-permute-start(bf16[400,128]{1,0:T(8,128)(2,1)S(1)} %get-tuple-element.54), channel_id=1, source_target_pairs={{0,15},{1,10},{2,9},{3,12},{4,11},{5,14},{6,13},{7,8},{8,7},{9,2},... | collective-permute-start | bytes 307208 | tf_op jit(solution)/shard_map/ppermute | solution.py:40
  10.0 0.6 %shard_map.142 = (bf16[400,128]{1,0:T(8,128)(2,1)S(1)}, bf16[400,128]{1,0:T(8,128)(2,1)S(1)}, bf16[400,128]{1,0:T(8,128)(2,1)S(1)}, bf16[400,128]{1,0:T(8,128)(2,1)S(1)}) custom-call(bf16[1600,128]{1,0:T(8,128)(2,1)S(1)} %get-tuple-element.46.own_ref, s32[8,32]{1,0:T(8,128)S(1)} %get-tuple-element.55.lists_ref.refs_8_), custom_call_target="tpu_custom_call" | custom-call | tf_op jit(solution)/shard_map/pallas_call | solution.py:383
  10.6 1.8 %collective-permute-start.4 = (bf16[400,128]{1,0:T(8,128)(2,1)S(1)}, bf16[400,128]{1,0:T(8,128)(2,1)S(1)}, u32[]{:S(2)}, u32[]{:S(2)}) collective-permute-start(bf16[400,128]{1,0:T(8,128)(2,1)S(1)} %get-tuple-element.56), channel_id=1, source_target_pairs={{0,25},{1,24},{2,27},{3,26},{4,29},{5,28},{6,31},{7,30},{8,17},{9,... | collective-permute-start | bytes 307208 | tf_op jit(solution)/shard_map/ppermute | solution.py:40
  12.4 0.0 collective-permute-done.refs_0_
  12.4 1.7 %collective-permute-start.5 = (bf16[400,128]{1,0:T(8,128)(2,1)S(1)}, bf16[400,128]{1,0:T(8,128)(2,1)S(1)}, u32[]{:S(2)}, u32[]{:S(2)}) collective-permute-start(bf16[400,128]{1,0:T(8,128)(2,1)S(1)} %get-tuple-element.57), channel_id=1, source_target_pairs={{0,9},{1,8},{2,11},{3,10},{4,13},{5,12},{6,15},{7,14},{8,1},{9,0},... | collective-permute-start | bytes 307208 | tf_op jit(solution)/shard_map/ppermute | solution.py:40
  14.1 0.6 %collective-permute-done.1.refs_1_ = bf16[400,128]{1,0:T(8,128)(2,1)S(1)} collective-permute-done((bf16[400,128]{1,0:T(8,128)(2,1)S(1)}, bf16[400,128]{1,0:T(8,128)(2,1)S(1)}, u32[]{:S(2)}, u32[]{:S(2)}) %collective-permute-start.1) | collective-permute-done | bytes 102432 | tf_op jit(solution)/shard_map/ppermute | solution.py:40
  14.6 1.0 %collective-permute-start.6 = (bf16[400,128]{1,0:T(8,128)(2,1)S(1)}, bf16[400,128]{1,0:T(8,128)(2,1)S(1)}, u32[]{:S(2)}, u32[]{:S(2)}) collective-permute-start(bf16[400,128]{1,0:T(8,128)(2,1)S(1)} %get-tuple-element.58), channel_id=1, source_target_pairs={{0,7},{1,2},{2,1},{3,4},{4,3},{5,6},{6,5},{7,0},{8,15},{9,10},{10,... | collective-permute-start | bytes 307208 | tf_op jit(solution)/shard_map/ppermute | solution.py:40
  15.7 0.4 collective-permute-done.2.refs_2_
  16.1 0.9 %collective-permute-start.7 = (bf16[400,128]{1,0:T(8,128)(2,1)S(1)}, bf16[400,128]{1,0:T(8,128)(2,1)S(1)}, u32[]{:S(2)}, u32[]{:S(2)}) collective-permute-start(bf16[400,128]{1,0:T(8,128)(2,1)S(1)} %get-tuple-element.59), channel_id=1, source_target_pairs={{0,1},{1,0},{2,3},{3,2},{4,5},{5,4},{6,7},{7,6},{8,9},{9,8},{10,11... | collective-permute-start | bytes 307208 | tf_op jit(solution)/shard_map/ppermute | solution.py:40
  16.9 4.2 %shard_map.141 = (f32[4,832,256]{2,1,0:T(8,128)S(1)}, f32[4,832,256]{2,1,0:T(8,128)S(1)}, f32[4,832,256]{2,1,0:T(8,128)S(1)}, bf16[4,200,200]{2,1,0:T(8,128)(2,1...) custom-call(bf16[1600,128]{1,0:T(8,128)(2,1)S(1)} %get-tuple-element, ...), custom_call_target="tpu_custom_call" | custom-call | tf_op jit(solution)/shard_map/pallas_call | solution.py:383
  21.1 0.0 collective-permute-done.3.refs_3_
  21.2 0.0 collective-permute-done.4.refs_4_
  21.2 0.0 collective-permute-done.5.refs_5_
  21.2 0.0 collective-permute-done.6.refs_6_
  21.2 0.0 collective-permute-done.7.refs_7_
  21.2 3.7 %shard_map.143 = (bf16[400,128]{1,0:T(8,128)(2,1)S(1)}, bf16[400,128]{1,0:T(8,128)(2,1)S(1)}, bf16[400,128]{1,0:T(8,128)(2,1)S(1)}, bf16[400,128]{1,0:T(8,128)(2...) custom-call(bf16[400,128]{1,0:T(8,128)(2,1)S(1)} %collective-permute-done.refs_0_, ...), custom_call_target="tpu_custom_call" | custom-call | tf_op jit(solution)/shard_map/pallas_call | solution.py:383
  24.9 3.1 %collective-permute-start.8 = (bf16[400,128]{1,0:T(8,128)(2,1)S(1)}, bf16[400,128]{1,0:T(8,128)(2,1)S(1)}, u32[]{:S(2)}, u32[]{:S(2)}) collective-permute-start(bf16[400,128]{1,0:T(8,128)(2,1)S(1)} %get-tuple-element.81), channel_id=1, source_target_pairs={{0,24},{1,25},{2,26},{3,27},{4,28},{5,29},{6,30},{7,31},{8,16},{9,... | collective-permute-start | bytes 307208 | tf_op jit(solution)/shard_map/ppermute | solution.py:40
  28.0 0.0 collective-permute-start.9
  28.0 2.3 %collective-permute-start.10 = (bf16[400,128]{1,0:T(8,128)(2,1)S(1)}, bf16[400,128]{1,0:T(8,128)(2,1)S(1)}, u32[]{:S(2)}, u32[]{:S(2)}) collective-permute-start(bf16[400,128]{1,0:T(8,128)(2,1)S(1)} %get-tuple-element.83), channel_id=1, source_target_pairs={{0,31},{1,26},{2,25},{3,28},{4,27},{5,30},{6,29},{7,24},{8,23},{9,... | collective-permute-start | bytes 307208 | tf_op jit(solution)/shard_map/ppermute | solution.py:40
  30.3 0.4 shard_map.145
  30.8 1.2 %collective-permute-start.11 = (bf16[400,128]{1,0:T(8,128)(2,1)S(1)}, bf16[400,128]{1,0:T(8,128)(2,1)S(1)}, u32[]{:S(2)}, u32[]{:S(2)}) collective-permute-start(bf16[400,128]{1,0:T(8,128)(2,1)S(1)} %get-tuple-element.84), channel_id=1, source_target_pairs={{0,15},{1,10},{2,9},{3,12},{4,11},{5,14},{6,13},{7,8},{8,7},{9,2},... | collective-permute-start | bytes 307208 | tf_op jit(solution)/shard_map/ppermute | solution.py:40
  31.9 1.2 %collective-permute-start.12 = (bf16[400,128]{1,0:T(8,128)(2,1)S(1)}, bf16[400,128]{1,0:T(8,128)(2,1)S(1)}, u32[]{:S(2)}, u32[]{:S(2)}) collective-permute-start(bf16[400,128]{1,0:T(8,128)(2,1)S(1)} %get-tuple-element.85), channel_id=1, source_target_pairs={{0,25},{1,24},{2,27},{3,26},{4,29},{5,28},{6,31},{7,30},{8,17},{9,... | collective-permute-start | bytes 307208 | tf_op jit(solution)/shard_map/ppermute | solution.py:40
  33.1 0.0 collective-permute-done.8.refs_0_
  33.1 1.6 %collective-permute-start.13 = (bf16[400,128]{1,0:T(8,128)(2,1)S(1)}, bf16[400,128]{1,0:T(8,128)(2,1)S(1)}, u32[]{:S(2)}, u32[]{:S(2)}) collective-permute-start(bf16[400,128]{1,0:T(8,128)(2,1)S(1)} %get-tuple-element.86), channel_id=1, source_target_pairs={{0,9},{1,8},{2,11},{3,10},{4,13},{5,12},{6,15},{7,14},{8,1},{9,0},... | collective-permute-start | bytes 307208 | tf_op jit(solution)/shard_map/ppermute | solution.py:40
  34.7 1.5 %collective-permute-done.9.refs_1_ = bf16[400,128]{1,0:T(8,128)(2,1)S(1)} collective-permute-done((bf16[400,128]{1,0:T(8,128)(2,1)S(1)}, bf16[400,128]{1,0:T(8,128)(2,1)S(1)}, u32[]{:S(2)}, u32[]{:S(2)}) %collective-permute-start.9) | collective-permute-done | bytes 102432 | tf_op jit(solution)/shard_map/ppermute | solution.py:40
  36.2 0.2 collective-permute-start.14
  36.5 0.8 %collective-permute-done.10.refs_2_ = bf16[400,128]{1,0:T(8,128)(2,1)S(1)} collective-permute-done((bf16[400,128]{1,0:T(8,128)(2,1)S(1)}, bf16[400,128]{1,0:T(8,128)(2,1)S(1)}, u32[]{:S(2)}, u32[]{:S(2)}) %collective-permute-start.10) | collective-permute-done | bytes 102432 | tf_op jit(solution)/shard_map/ppermute | solution.py:40
  37.3 0.6 %collective-permute-start.15 = (bf16[400,128]{1,0:T(8,128)(2,1)S(1)}, bf16[400,128]{1,0:T(8,128)(2,1)S(1)}, u32[]{:S(2)}, u32[]{:S(2)}) collective-permute-start(bf16[400,128]{1,0:T(8,128)(2,1)S(1)} %get-tuple-element.88), channel_id=1, source_target_pairs={{0,1},{1,0},{2,3},{3,2},{4,5},{5,4},{6,7},{7,6},{8,9},{9,8},{10,11... | collective-permute-start | bytes 307208 | tf_op jit(solution)/shard_map/ppermute | solution.py:40
  37.9 4.0 %shard_map.144 = (bf16[25,4,16,128]{3,2,1,0:T(8,128)(2,1)}, f32[25,8,8,128]{3,2,1,0:T(8,128)S(1)}) custom-call(bf16[1600,128]{1,0:T(8,128)(2,1)S(1)} %get-tuple-element.46.own_ref, bf16[1600,128]{1,0:T(8,128)(2,1)S(1)} %get-tuple-element.47.cot_ref, s32[1,256]{1,0:T(1,128)S(1)} %get-tuple-element.48.src_ref, ...), custom_call_target="tpu_custom_call" | custom-call | tf_op jit(solution)/shard_map/pallas_call | solution.py:383
  41.9 0.0 collective-permute-done.11.refs_3_
  41.9 0.0 collective-permute-done.12.refs_4_
  41.9 0.5 %collective-permute-done.13.refs_5_ = bf16[400,128]{1,0:T(8,128)(2,1)S(1)} collective-permute-done((bf16[400,128]{1,0:T(8,128)(2,1)S(1)}, bf16[400,128]{1,0:T(8,128)(2,1)S(1)}, u32[]{:S(2)}, u32[]{:S(2)}) %collective-permute-start.13) | collective-permute-done | bytes 102432 | tf_op jit(solution)/shard_map/ppermute | solution.py:40
  42.4 0.0 collective-permute-done.14.refs_6_
  42.4 0.0 collective-permute-done.15.refs_7_
  42.4 1.5 %shard_map.146 = f32[25,64,128]{2,1,0:T(8,128)} custom-call(bf16[400,128]{1,0:T(8,128)(2,1)S(1)} %collective-permute-done.8.refs_0_, bf16[400,128]{1,0:T(8,128)(2,1)S(1)} %collective-permute-done.9.refs_1_, bf16[400,128]{1,0:T(8,128)(2,1)S(1)} %collective-permute-done.10.refs_2_, bf16[400,128]{1,0:T(8,128)(2,1)S(1)} %collective-permute-done.11.refs_3_, ...), custom_call_target="tpu_custom_call" | custom-call | tf_op jit(solution)/shard_map/pallas_call | solution.py:383
Async XLA Ops:
  2.0 10.3 %collective-permute-start = (bf16[400,128]{1,0:T(8,128)(2,1)S(1)}, bf16[400,128]{1,0:T(8,128)(2,1)S(1)}, u32[]{:S(2)}, u32[]{:S(2)}) collective-permute-start(bf16[400,128]{1,0:T(8,128)(2,1)S(1)} %get-tuple-element.51), channel_id=1, source_target_pairs={{0,24},{1,25},{2,26},{3,27},{4,28},{5,29},{6,30},{7,31},{8,16},{9,... | collective-permute-start | bytes 307208 | tf_op jit(solution)/shard_map/ppermute | solution.py:40
  7.2 7.5 %collective-permute-start.1 = (bf16[400,128]{1,0:T(8,128)(2,1)S(1)}, bf16[400,128]{1,0:T(8,128)(2,1)S(1)}, u32[]{:S(2)}, u32[]{:S(2)}) collective-permute-start(bf16[400,128]{1,0:T(8,128)(2,1)S(1)} %get-tuple-element.52), channel_id=1, source_target_pairs={{0,8},{1,9},{2,10},{3,11},{4,12},{5,13},{6,14},{7,15},{8,0},{9,1},... | collective-permute-start | bytes 307208 | tf_op jit(solution)/shard_map/ppermute | solution.py:40
  7.2 8.9 %collective-permute-start.2 = (bf16[400,128]{1,0:T(8,128)(2,1)S(1)}, bf16[400,128]{1,0:T(8,128)(2,1)S(1)}, u32[]{:S(2)}, u32[]{:S(2)}) collective-permute-start(bf16[400,128]{1,0:T(8,128)(2,1)S(1)} %get-tuple-element.53), channel_id=1, source_target_pairs={{0,31},{1,26},{2,25},{3,28},{4,27},{5,30},{6,29},{7,24},{8,23},{9,... | collective-permute-start | bytes 307208 | tf_op jit(solution)/shard_map/ppermute | solution.py:40
  8.8 12.3 %collective-permute-start.3 = (bf16[400,128]{1,0:T(8,128)(2,1)S(1)}, bf16[400,128]{1,0:T(8,128)(2,1)S(1)}, u32[]{:S(2)}, u32[]{:S(2)}) collective-permute-start(bf16[400,128]{1,0:T(8,128)(2,1)S(1)} %get-tuple-element.54), channel_id=1, source_target_pairs={{0,15},{1,10},{2,9},{3,12},{4,11},{5,14},{6,13},{7,8},{8,7},{9,2},... | collective-permute-start | bytes 307208 | tf_op jit(solution)/shard_map/ppermute | solution.py:40
  10.6 10.6 %collective-permute-start.4 = (bf16[400,128]{1,0:T(8,128)(2,1)S(1)}, bf16[400,128]{1,0:T(8,128)(2,1)S(1)}, u32[]{:S(2)}, u32[]{:S(2)}) collective-permute-start(bf16[400,128]{1,0:T(8,128)(2,1)S(1)} %get-tuple-element.56), channel_id=1, source_target_pairs={{0,25},{1,24},{2,27},{3,26},{4,29},{5,28},{6,31},{7,30},{8,17},{9,... | collective-permute-start | bytes 307208 | tf_op jit(solution)/shard_map/ppermute | solution.py:40
  12.4 8.8 %collective-permute-start.5 = (bf16[400,128]{1,0:T(8,128)(2,1)S(1)}, bf16[400,128]{1,0:T(8,128)(2,1)S(1)}, u32[]{:S(2)}, u32[]{:S(2)}) collective-permute-start(bf16[400,128]{1,0:T(8,128)(2,1)S(1)} %get-tuple-element.57), channel_id=1, source_target_pairs={{0,9},{1,8},{2,11},{3,10},{4,13},{5,12},{6,15},{7,14},{8,1},{9,0},... | collective-permute-start | bytes 307208 | tf_op jit(solution)/shard_map/ppermute | solution.py:40
  14.6 6.5 %collective-permute-start.6 = (bf16[400,128]{1,0:T(8,128)(2,1)S(1)}, bf16[400,128]{1,0:T(8,128)(2,1)S(1)}, u32[]{:S(2)}, u32[]{:S(2)}) collective-permute-start(bf16[400,128]{1,0:T(8,128)(2,1)S(1)} %get-tuple-element.58), channel_id=1, source_target_pairs={{0,7},{1,2},{2,1},{3,4},{4,3},{5,6},{6,5},{7,0},{8,15},{9,10},{10,... | collective-permute-start | bytes 307208 | tf_op jit(solution)/shard_map/ppermute | solution.py:40
  16.1 5.1 %collective-permute-start.7 = (bf16[400,128]{1,0:T(8,128)(2,1)S(1)}, bf16[400,128]{1,0:T(8,128)(2,1)S(1)}, u32[]{:S(2)}, u32[]{:S(2)}) collective-permute-start(bf16[400,128]{1,0:T(8,128)(2,1)S(1)} %get-tuple-element.59), channel_id=1, source_target_pairs={{0,1},{1,0},{2,3},{3,2},{4,5},{5,4},{6,7},{7,6},{8,9},{9,8},{10,11... | collective-permute-start | bytes 307208 | tf_op jit(solution)/shard_map/ppermute | solution.py:40
  24.9 8.2 %collective-permute-start.8 = (bf16[400,128]{1,0:T(8,128)(2,1)S(1)}, bf16[400,128]{1,0:T(8,128)(2,1)S(1)}, u32[]{:S(2)}, u32[]{:S(2)}) collective-permute-start(bf16[400,128]{1,0:T(8,128)(2,1)S(1)} %get-tuple-element.81), channel_id=1, source_target_pairs={{0,24},{1,25},{2,26},{3,27},{4,28},{5,29},{6,30},{7,31},{8,16},{9,... | collective-permute-start | bytes 307208 | tf_op jit(solution)/shard_map/ppermute | solution.py:40
  28.0 8.2 %collective-permute-start.9 = (bf16[400,128]{1,0:T(8,128)(2,1)S(1)}, bf16[400,128]{1,0:T(8,128)(2,1)S(1)}, u32[]{:S(2)}, u32[]{:S(2)}) collective-permute-start(bf16[400,128]{1,0:T(8,128)(2,1)S(1)} %get-tuple-element.82), channel_id=1, source_target_pairs={{0,8},{1,9},{2,10},{3,11},{4,12},{5,13},{6,14},{7,15},{8,0},{9,1},... | collective-permute-start | bytes 307208 | tf_op jit(solution)/shard_map/ppermute | solution.py:40
  28.0 9.2 %collective-permute-start.10 = (bf16[400,128]{1,0:T(8,128)(2,1)S(1)}, bf16[400,128]{1,0:T(8,128)(2,1)S(1)}, u32[]{:S(2)}, u32[]{:S(2)}) collective-permute-start(bf16[400,128]{1,0:T(8,128)(2,1)S(1)} %get-tuple-element.83), channel_id=1, source_target_pairs={{0,31},{1,26},{2,25},{3,28},{4,27},{5,30},{6,29},{7,24},{8,23},{9,... | collective-permute-start | bytes 307208 | tf_op jit(solution)/shard_map/ppermute | solution.py:40
  30.8 11.2 %collective-permute-start.11 = (bf16[400,128]{1,0:T(8,128)(2,1)S(1)}, bf16[400,128]{1,0:T(8,128)(2,1)S(1)}, u32[]{:S(2)}, u32[]{:S(2)}) collective-permute-start(bf16[400,128]{1,0:T(8,128)(2,1)S(1)} %get-tuple-element.84), channel_id=1, source_target_pairs={{0,15},{1,10},{2,9},{3,12},{4,11},{5,14},{6,13},{7,8},{8,7},{9,2},... | collective-permute-start | bytes 307208 | tf_op jit(solution)/shard_map/ppermute | solution.py:40
  31.9 10.0 %collective-permute-start.12 = (bf16[400,128]{1,0:T(8,128)(2,1)S(1)}, bf16[400,128]{1,0:T(8,128)(2,1)S(1)}, u32[]{:S(2)}, u32[]{:S(2)}) collective-permute-start(bf16[400,128]{1,0:T(8,128)(2,1)S(1)} %get-tuple-element.85), channel_id=1, source_target_pairs={{0,25},{1,24},{2,27},{3,26},{4,29},{5,28},{6,31},{7,30},{8,17},{9,... | collective-permute-start | bytes 307208 | tf_op jit(solution)/shard_map/ppermute | solution.py:40
  33.1 9.3 %collective-permute-start.13 = (bf16[400,128]{1,0:T(8,128)(2,1)S(1)}, bf16[400,128]{1,0:T(8,128)(2,1)S(1)}, u32[]{:S(2)}, u32[]{:S(2)}) collective-permute-start(bf16[400,128]{1,0:T(8,128)(2,1)S(1)} %get-tuple-element.86), channel_id=1, source_target_pairs={{0,9},{1,8},{2,11},{3,10},{4,13},{5,12},{6,15},{7,14},{8,1},{9,0},... | collective-permute-start | bytes 307208 | tf_op jit(solution)/shard_map/ppermute | solution.py:40
  36.2 6.2 %collective-permute-start.14 = (bf16[400,128]{1,0:T(8,128)(2,1)S(1)}, bf16[400,128]{1,0:T(8,128)(2,1)S(1)}, u32[]{:S(2)}, u32[]{:S(2)}) collective-permute-start(bf16[400,128]{1,0:T(8,128)(2,1)S(1)} %get-tuple-element.87), channel_id=1, source_target_pairs={{0,7},{1,2},{2,1},{3,4},{4,3},{5,6},{6,5},{7,0},{8,15},{9,10},{10,... | collective-permute-start | bytes 307208 | tf_op jit(solution)/shard_map/ppermute | solution.py:40
  37.3 5.2 %collective-permute-start.15 = (bf16[400,128]{1,0:T(8,128)(2,1)S(1)}, bf16[400,128]{1,0:T(8,128)(2,1)S(1)}, u32[]{:S(2)}, u32[]{:S(2)}) collective-permute-start(bf16[400,128]{1,0:T(8,128)(2,1)S(1)} %get-tuple-element.88), channel_id=1, source_target_pairs={{0,1},{1,0},{2,3},{3,2},{4,5},{5,4},{6,7},{7,6},{8,9},{9,8},{10,11... | collective-permute-start | bytes 307208 | tf_op jit(solution)/shard_map/ppermute | solution.py:40

commit v2 on v1

--- a/solution.py
+++ b/solution.py
@@ -10,7 +10,7 @@
 COEFS = 25
 DEGREES = 5
 edge_norm = 0.35
-SWAPS = ((1, None), (0, None), (1, 1), (0, 1), (1, 0), (0, 0), (None, 1), (None, 0))
+SWAPS = ((0, None), (1, None), (1, 1), (0, 1), (1, 0), (0, 0), (None, 1), (None, 0))
 
 
 def step_of(axis, parity):
@@ -72,24 +72,14 @@
     return result
 
 
-def lent_lists(lists, atoms):
-    place = iota((8, 8), 0)
-    wanted = jnp.zeros((8, 8), I32)
-    for s, swap in enumerate(SWAPS):
-        wanted = jnp.where(place == s, 7 - received_direction(swap), wanted)
-    order = (wanted == iota((8, 8), 1)).astype(BF16)
-    ghost = lists.shape[1]
-    spread = (lax.rem(iota((ghost, atoms), 1), ghost) == iota((ghost, atoms), 0)).astype(BF16)
-    chosen = dot(order, lists.astype(F32).astype(BF16)).astype(BF16)
-    return dot(chosen, spread).astype(I32)
-
-
-def lent_pick(lists, q, groups):
-    atoms = lists.shape[1]
-    row = jnp.concatenate(
-        [merged([lists[4 * g + k : 4 * g + k + 1] for k in range(4)], q) for g in groups], axis=1
-    )
-    return (iota((atoms, row.shape[1]), 0) == row).astype(BF16)
+def lent_lists(lists_ref, swaps):
+    rows = [lists_ref[pl.ds(7 - received_direction(swap), 1), :] for swap in swaps]
+    return [jnp.concatenate([row] * 4, axis=1) for row in rows]
+
+
+def lent_pick(lists, q):
+    row = merged(lists, q)
+    return (iota((row.shape[1], row.shape[1]), 0) == row).astype(BF16)
 
 
 def fetch(sources, targets, sems):
@@ -99,9 +89,9 @@
     return copies
 
 
-def pack_group(own, lists, outs, scratch, g):
-    for q in range(4):
-        scratch[q] = dot(rows_of(own, q), lent_pick(lists, q, (g,)))
+def pack_group(own, lists, outs, scratch):
+    for q in range(4):
+        scratch[q] = dot(rows_of(own, q), lent_pick(lists, q))
     for k in range(4):
         outs[k][...] = merged([scratch[q] for q in range(4)], k).astype(BF16)
 
@@ -110,14 +100,13 @@
     outs, own_ref, lists_ref, scratch, sems = refs[:4], refs[4], refs[5], refs[6], refs[7]
     copies = fetch((lists_hbm, own_hbm), (lists_ref, own_ref), sems)
     copies[0].wait()
-    lists = lent_lists(lists_ref[...], own_ref.shape[1])
+    lists = lent_lists(lists_ref, SWAPS[:4])
     copies[1].wait()
-    pack_group(own_ref[...], lists, outs, scratch, 0)
+    pack_group(own_ref[...], lists, outs, scratch)
 
 
 def pack_rest_kernel(own_ref, lists_ref, *refs):
-    lists = lent_lists(lists_ref[...], own_ref.shape[1])
-    pack_group(own_ref[...], lists, refs[:4], refs[4], 1)
+    pack_group(own_ref[...], lent_lists(lists_ref, SWAPS[4:]), refs[:4], refs[4])
 
 
 def equal_bits(shape, axis_shift, other_shift):
@@ -328,13 +317,20 @@
     return_group(dsrc_ref, picks_ref, refs[:4], refs[4], 1)
 
 
-def after_kernel(own_ref, cot_ref, src_ref, down_ref, fdown_ref, act_ref, feat_ref, prod_ref, dsrc_ref, out_ref, grad_ref):
+def after_kernel(*refs):
+    own_ref, cot_ref, src_ref, lists_ref, down_ref, fdown_ref = refs[:6]
+    act_ref, feat_ref, prod_ref, dsrc_ref, out_ref, grad_ref, lent_ref = refs[6:]
     rows, atoms = own_ref.shape
     channels = rows // COEFS
     edges = src_ref.shape[1]
     own_pick = (iota((atoms, edges), 0) == src_ref[...]).astype(BF16)
     own = own_ref[...].astype(F32).reshape(COEFS, channels // 8, 8, atoms)
     cot = cot_ref[...].astype(F32).reshape(COEFS, channels // 8, 8, atoms)
+
+    for g in range(2):
+        lists = lent_lists(lists_ref, SWAPS[4 * g : 4 * g + 4])
+        for q in range(4):
+            lent_ref[q, :, g * atoms : (g + 1) * atoms] = lent_pick(lists, q)
 
     def down(parts, value):
         high, low = split(value)
@@ -357,13 +353,12 @@
 
 def final_kernel(*refs):
     blocks = [r[...] for r in refs[:8]]
-    lists_ref, grad_ref, out_hbm, total, sems = refs[8:]
+    lent_ref, grad_ref, out_hbm, total, sems = refs[8:]
     atoms = grad_ref.shape[2]
-    lists = lent_lists(lists_ref[...], atoms)
     copies = []
     for q in range(4):
         taken = jnp.concatenate([merged(blocks[4 * g : 4 * g + 4], q) for g in range(2)], axis=1)
-        added = dot_nt(taken, lent_pick(lists, q, (0, 1)))
+        added = dot_nt(taken, lent_ref[q])
         quarter = added.shape[0] // COEFS
         here = slice(q * quarter, (q + 1) * quarter)
         total[:, here] = grad_ref[:, here] + added.reshape(COEFS, quarter, atoms)
@@ -474,16 +469,20 @@
     )(*ghosts, *direct, *turned, picks, both, part, harm, gate, up, down)
     returns += call(edge_rest_kernel, [block] * 4, [pltpu.VMEM((4, rows // 4, atoms), BF16)])(dsrc, picks)
     arrived = [traded(returns[s], swap) for s, swap in enumerate(SWAPS)]
-    layer, grad = call(
+    layer, grad, lent = call(
         after_kernel,
-        [like((COEFS, pairs, 16, atoms), BF16), like((COEFS, channels // 8, 8, atoms), F32)],
-    )(own, cot, src, down, fdown, act, feat, prod, dsrc)
+        [
+            like((COEFS, pairs, 16, atoms), BF16),
+            like((COEFS, channels // 8, 8, atoms), F32),
+            like((4, atoms, 2 * atoms), BF16),
+        ],
+    )(own, cot, src, lists, down, fdown, act, feat, prod, dsrc)
     total = call(
         final_kernel,
         pltpu.HBM((COEFS, channels, atoms), F32),
         [pltpu.VMEM((COEFS, channels, atoms), F32), pltpu.SemaphoreType.DMA((4,))],
         out_spec=HB,
-    )(*arrived, lists, grad.reshape(COEFS, channels, atoms))
+    )(*arrived, lent, grad.reshape(COEFS, channels, atoms))
     return layer.reshape(1, 1, rows, atoms), total.reshape(1, 1, rows, atoms)
 
 

time: 44.2 us -> 47.9 us (1.084)
  the two profiles are of different devices: /device:TPU:0 before, /device:TPU:19 now
where the time goes in v2:
time: 47.9 us; the launch traced here: 47.7 us
  starting transfers between devices  24.2 us (51%)
  Pallas kernels  15.5 us (32%)
  waiting for transfers between devices  7.26 us (15%)
  between operations  0.75 us (2%)
    ppermute x16, starting transfers between devices, traded(): return lax.ppermute(value, ('gx', 'gy'), pairs)  24.2 us
    pallas_call x7, Pallas kernels, run(): pl.pallas_call(kernel, out_shape=outs, in_specs=[HB if n in far else VM f...  15.5 us
    ppermute x16, waiting for transfers between devices, traded(): return lax.ppermute(value, ('gx', 'gy'), pairs)  7.26 us
  transfers between devices with their start and end apart: 16, of which 3 were waited for; matrix products, arithmetic and copies ran while one was open for 0% of the time, Pallas kernels for 19%

profile of v2, /device:TPU:19, one launch (start us, length us, event | category | flops | bytes accessed | tf_op | source)
XLA Modules:
  0.0 47.7 jit_solution(10563995323917468297)
XLA Ops:
  0.6 1.4 %shard_map.140 = (bf16[400,128]{1,0:T(8,128)(2,1)S(1)}, bf16[400,128]{1,0:T(8,128)(2,1)S(1)}, bf16[400,128]{1,0:T(8,128)(2,1)S(1)}, bf16[400,128]{1,0:T(8,128)(2...) custom-call(bf16[1600,128]{1,0:T(8,128)(2,1)} %bitcast.12, s32[8,32]{1,0:T(8,128)} %bitcast.16), custom_call_target="tpu_custom_call" | custom-call | tf_op jit(solution)/shard_map/pallas_call | solution.py:378
  2.0 1.4 %collective-permute-start = (bf16[400,128]{1,0:T(8,128)(2,1)S(1)}, bf16[400,128]{1,0:T(8,128)(2,1)S(1)}, u32[]{:S(2)}, u32[]{:S(2)}) collective-permute-start(bf16[400,128]{1,0:T(8,128)(2,1)S(1)} %get-tuple-element.53), channel_id=1, source_target_pairs={{0,8},{1,9},{2,10},{3,11},{4,12},{5,13},{6,14},{7,15},{8,0},{9,1},... | collective-permute-start | bytes 307208 | tf_op jit(solution)/shard_map/ppermute | solution.py:40
  3.4 0.0 collective-permute-start.1
  3.4 3.5 %collective-permute-start.2 = (bf16[400,128]{1,0:T(8,128)(2,1)S(1)}, bf16[400,128]{1,0:T(8,128)(2,1)S(1)}, u32[]{:S(2)}, u32[]{:S(2)}) collective-permute-start(bf16[400,128]{1,0:T(8,128)(2,1)S(1)} %get-tuple-element.55), channel_id=1, source_target_pairs={{0,31},{1,26},{2,25},{3,28},{4,27},{5,30},{6,29},{7,24},{8,23},{9,... | collective-permute-start | bytes 307208 | tf_op jit(solution)/shard_map/ppermute | solution.py:40
  6.9 2.0 %collective-permute-start.3 = (bf16[400,128]{1,0:T(8,128)(2,1)S(1)}, bf16[400,128]{1,0:T(8,128)(2,1)S(1)}, u32[]{:S(2)}, u32[]{:S(2)}) collective-permute-start(bf16[400,128]{1,0:T(8,128)(2,1)S(1)} %get-tuple-element.56), channel_id=1, source_target_pairs={{0,15},{1,10},{2,9},{3,12},{4,11},{5,14},{6,13},{7,8},{8,7},{9,2},... | collective-permute-start | bytes 307208 | tf_op jit(solution)/shard_map/ppermute | solution.py:40
  8.9 0.4 shard_map.142
  9.4 0.5 collective-permute-start.4
  9.8 0.0 collective-permute-done.refs_0_
  9.8 0.9 %collective-permute-start.5 = (bf16[400,128]{1,0:T(8,128)(2,1)S(1)}, bf16[400,128]{1,0:T(8,128)(2,1)S(1)}, u32[]{:S(2)}, u32[]{:S(2)}) collective-permute-start(bf16[400,128]{1,0:T(8,128)(2,1)S(1)} %get-tuple-element.58), channel_id=1, source_target_pairs={{0,9},{1,8},{2,11},{3,10},{4,13},{5,12},{6,15},{7,14},{8,1},{9,0},... | collective-permute-start | bytes 307208 | tf_op jit(solution)/shard_map/ppermute | solution.py:40
  10.8 0.6 %collective-permute-done.1.refs_1_ = bf16[400,128]{1,0:T(8,128)(2,1)S(1)} collective-permute-done((bf16[400,128]{1,0:T(8,128)(2,1)S(1)}, bf16[400,128]{1,0:T(8,128)(2,1)S(1)}, u32[]{:S(2)}, u32[]{:S(2)}) %collective-permute-start.1) | collective-permute-done | bytes 102432 | tf_op jit(solution)/shard_map/ppermute | solution.py:40
  11.3 4.1 %collective-permute-start.6 = (bf16[400,128]{1,0:T(8,128)(2,1)S(1)}, bf16[400,128]{1,0:T(8,128)(2,1)S(1)}, u32[]{:S(2)}, u32[]{:S(2)}) collective-permute-start(bf16[400,128]{1,0:T(8,128)(2,1)S(1)} %get-tuple-element.59), channel_id=1, source_target_pairs={{0,7},{1,2},{2,1},{3,4},{4,3},{5,6},{6,5},{7,0},{8,15},{9,10},{10,... | collective-permute-start | bytes 307208 | tf_op jit(solution)/shard_map/ppermute | solution.py:40
  15.4 3.2 %collective-permute-done.2.refs_2_ = bf16[400,128]{1,0:T(8,128)(2,1)S(1)} collective-permute-done((bf16[400,128]{1,0:T(8,128)(2,1)S(1)}, bf16[400,128]{1,0:T(8,128)(2,1)S(1)}, u32[]{:S(2)}, u32[]{:S(2)}) %collective-permute-start.2) | collective-permute-done | bytes 102432 | tf_op jit(solution)/shard_map/ppermute | solution.py:40
  18.6 0.0 collective-permute-start.7
  18.6 4.2 %shard_map.141 = (f32[4,832,256]{2,1,0:T(8,128)S(1)}, f32[4,832,256]{2,1,0:T(8,128)S(1)}, f32[4,832,256]{2,1,0:T(8,128)S(1)}, bf16[4,200,200]{2,1,0:T(8,128)(2,1...) custom-call(bf16[1600,128]{1,0:T(8,128)(2,1)S(1)} %get-tuple-element, ...), custom_call_target="tpu_custom_call" | custom-call | tf_op jit(solution)/shard_map/pallas_call | solution.py:378
  22.9 0.0 collective-permute-done.3.refs_3_
  22.9 0.0 collective-permute-done.4.refs_4_
  22.9 0.0 collective-permute-done.5.refs_5_
  22.9 0.0 collective-permute-done.6.refs_6_
  22.9 0.0 collective-permute-done.7.refs_7_
  22.9 3.7 %shard_map.143 = (bf16[400,128]{1,0:T(8,128)(2,1)S(1)}, bf16[400,128]{1,0:T(8,128)(2,1)S(1)}, bf16[400,128]{1,0:T(8,128)(2,1)S(1)}, bf16[400,128]{1,0:T(8,128)(2...) custom-call(bf16[400,128]{1,0:T(8,128)(2,1)S(1)} %collective-permute-done.refs_0_, ...), custom_call_target="tpu_custom_call" | custom-call | tf_op jit(solution)/shard_map/pallas_call | solution.py:378
  26.6 0.1 collective-permute-start.8
  26.7 0.1 collective-permute-start.9
  26.8 3.3 %collective-permute-start.10 = (bf16[400,128]{1,0:T(8,128)(2,1)S(1)}, bf16[400,128]{1,0:T(8,128)(2,1)S(1)}, u32[]{:S(2)}, u32[]{:S(2)}) collective-permute-start(bf16[400,128]{1,0:T(8,128)(2,1)S(1)} %get-tuple-element.84), channel_id=1, source_target_pairs={{0,31},{1,26},{2,25},{3,28},{4,27},{5,30},{6,29},{7,24},{8,23},{9,... | collective-permute-start | bytes 307208 | tf_op jit(solution)/shard_map/ppermute | solution.py:40
  30.1 0.4 shard_map.145
  30.6 3.4 %collective-permute-start.11 = (bf16[400,128]{1,0:T(8,128)(2,1)S(1)}, bf16[400,128]{1,0:T(8,128)(2,1)S(1)}, u32[]{:S(2)}, u32[]{:S(2)}) collective-permute-start(bf16[400,128]{1,0:T(8,128)(2,1)S(1)} %get-tuple-element.85), channel_id=1, source_target_pairs={{0,15},{1,10},{2,9},{3,12},{4,11},{5,14},{6,13},{7,8},{8,7},{9,2},... | collective-permute-start | bytes 307208 | tf_op jit(solution)/shard_map/ppermute | solution.py:40
  34.0 0.0 collective-permute-start.12
  34.0 0.0 collective-permute-done.8.refs_0_
  34.0 1.4 %collective-permute-start.13 = (bf16[400,128]{1,0:T(8,128)(2,1)S(1)}, bf16[400,128]{1,0:T(8,128)(2,1)S(1)}, u32[]{:S(2)}, u32[]{:S(2)}) collective-permute-start(bf16[400,128]{1,0:T(8,128)(2,1)S(1)} %get-tuple-element.87), channel_id=1, source_target_pairs={{0,9},{1,8},{2,11},{3,10},{4,13},{5,12},{6,15},{7,14},{8,1},{9,0},... | collective-permute-start | bytes 307208 | tf_op jit(solution)/shard_map/ppermute | solution.py:40
  35.4 0.0 collective-permute-done.9.refs_1_
  35.4 3.5 %collective-permute-start.14 = (bf16[400,128]{1,0:T(8,128)(2,1)S(1)}, bf16[400,128]{1,0:T(8,128)(2,1)S(1)}, u32[]{:S(2)}, u32[]{:S(2)}) collective-permute-start(bf16[400,128]{1,0:T(8,128)(2,1)S(1)} %get-tuple-element.88), channel_id=1, source_target_pairs={{0,7},{1,2},{2,1},{3,4},{4,3},{5,6},{6,5},{7,0},{8,15},{9,10},{10,... | collective-permute-start | bytes 307208 | tf_op jit(solution)/shard_map/ppermute | solution.py:40
  38.9 3.4 %collective-permute-done.10.refs_2_ = bf16[400,128]{1,0:T(8,128)(2,1)S(1)} collective-permute-done((bf16[400,128]{1,0:T(8,128)(2,1)S(1)}, bf16[400,128]{1,0:T(8,128)(2,1)S(1)}, u32[]{:S(2)}, u32[]{:S(2)}) %collective-permute-start.10) | collective-permute-done | bytes 102432 | tf_op jit(solution)/shard_map/ppermute | solution.py:40
  42.3 0.0 collective-permute-start.15
  42.3 4.1 %shard_map.144 = (bf16[25,4,16,128]{3,2,1,0:T(8,128)(2,1)}, f32[25,8,8,128]{3,2,1,0:T(8,128)S(1)}, bf16[4,128,256]{2,1,0:T(8,128)(2,1)S(1)}) custom-call(bf16[1600,128]{1,0:T(8,128)(2,1)S(1)} %get-tuple-element.47.own_ref.refs_0_, bf16[1600,128]{1,0:T(8,128)(2,1)S(1)} %get-tuple-element.48.refs_1_, s32[1,256]{1,0:T(1,128)S(1)} %get-tuple-element.49.refs_2_, ...), custom_call_target="tpu_custom_call" | custom-call | tf_op jit(solution)/shard_map/pallas_call | solution.py:378
  46.4 0.0 collective-permute-done.11.refs_3_
  46.4 0.0 collective-permute-done.12.refs_4_
  46.4 0.0 collective-permute-done.13.refs_5_
  46.4 0.0 collective-permute-done.14.refs_6_
  46.4 0.0 collective-permute-done.15.refs_7_
  46.4 1.2 %shard_map.146 = f32[25,64,128]{2,1,0:T(8,128)} custom-call(bf16[400,128]{1,0:T(8,128)(2,1)S(1)} %collective-permute-done.8.refs_0_, bf16[400,128]{1,0:T(8,128)(2,1)S(1)} %collective-permute-done.9.refs_1_, bf16[400,128]{1,0:T(8,128)(2,1)S(1)} %collective-permute-done.10.refs_2_, bf16[400,128]{1,0:T(8,128)(2,1)S(1)} %collective-permute-done.11.refs_3_, ...), custom_call_target="tpu_custom_call" | custom-call | tf_op jit(solution)/shard_map/pallas_call | solution.py:378
Async XLA Ops:
  2.0 7.8 %collective-permute-start = (bf16[400,128]{1,0:T(8,128)(2,1)S(1)}, bf16[400,128]{1,0:T(8,128)(2,1)S(1)}, u32[]{:S(2)}, u32[]{:S(2)}) collective-permute-start(bf16[400,128]{1,0:T(8,128)(2,1)S(1)} %get-tuple-element.53), channel_id=1, source_target_pairs={{0,8},{1,9},{2,10},{3,11},{4,12},{5,13},{6,14},{7,15},{8,0},{9,1},... | collective-permute-start | bytes 307208 | tf_op jit(solution)/shard_map/ppermute | solution.py:40
  3.4 7.9 %collective-permute-start.1 = (bf16[400,128]{1,0:T(8,128)(2,1)S(1)}, bf16[400,128]{1,0:T(8,128)(2,1)S(1)}, u32[]{:S(2)}, u32[]{:S(2)}) collective-permute-start(bf16[400,128]{1,0:T(8,128)(2,1)S(1)} %get-tuple-element.54), channel_id=1, source_target_pairs={{0,24},{1,25},{2,26},{3,27},{4,28},{5,29},{6,30},{7,31},{8,16},{9,... | collective-permute-start | bytes 307208 | tf_op jit(solution)/shard_map/ppermute | solution.py:40
  3.4 15.2 %collective-permute-start.2 = (bf16[400,128]{1,0:T(8,128)(2,1)S(1)}, bf16[400,128]{1,0:T(8,128)(2,1)S(1)}, u32[]{:S(2)}, u32[]{:S(2)}) collective-permute-start(bf16[400,128]{1,0:T(8,128)(2,1)S(1)} %get-tuple-element.55), channel_id=1, source_target_pairs={{0,31},{1,26},{2,25},{3,28},{4,27},{5,30},{6,29},{7,24},{8,23},{9,... | collective-permute-start | bytes 307208 | tf_op jit(solution)/shard_map/ppermute | solution.py:40
  6.9 16.0 %collective-permute-start.3 = (bf16[400,128]{1,0:T(8,128)(2,1)S(1)}, bf16[400,128]{1,0:T(8,128)(2,1)S(1)}, u32[]{:S(2)}, u32[]{:S(2)}) collective-permute-start(bf16[400,128]{1,0:T(8,128)(2,1)S(1)} %get-tuple-element.56), channel_id=1, source_target_pairs={{0,15},{1,10},{2,9},{3,12},{4,11},{5,14},{6,13},{7,8},{8,7},{9,2},... | collective-permute-start | bytes 307208 | tf_op jit(solution)/shard_map/ppermute | solution.py:40
  9.4 13.5 %collective-permute-start.4 = (bf16[400,128]{1,0:T(8,128)(2,1)S(1)}, bf16[400,128]{1,0:T(8,128)(2,1)S(1)}, u32[]{:S(2)}, u32[]{:S(2)}) collective-permute-start(bf16[400,128]{1,0:T(8,128)(2,1)S(1)} %get-tuple-element.57), channel_id=1, source_target_pairs={{0,25},{1,24},{2,27},{3,26},{4,29},{5,28},{6,31},{7,30},{8,17},{9,... | collective-permute-start | bytes 307208 | tf_op jit(solution)/shard_map/ppermute | solution.py:40
  9.8 13.1 %collective-permute-start.5 = (bf16[400,128]{1,0:T(8,128)(2,1)S(1)}, bf16[400,128]{1,0:T(8,128)(2,1)S(1)}, u32[]{:S(2)}, u32[]{:S(2)}) collective-permute-start(bf16[400,128]{1,0:T(8,128)(2,1)S(1)} %get-tuple-element.58), channel_id=1, source_target_pairs={{0,9},{1,8},{2,11},{3,10},{4,13},{5,12},{6,15},{7,14},{8,1},{9,0},... | collective-permute-start | bytes 307208 | tf_op jit(solution)/shard_map/ppermute | solution.py:40
  11.3 11.6 %collective-permute-start.6 = (bf16[400,128]{1,0:T(8,128)(2,1)S(1)}, bf16[400,128]{1,0:T(8,128)(2,1)S(1)}, u32[]{:S(2)}, u32[]{:S(2)}) collective-permute-start(bf16[400,128]{1,0:T(8,128)(2,1)S(1)} %get-tuple-element.59), channel_id=1, source_target_pairs={{0,7},{1,2},{2,1},{3,4},{4,3},{5,6},{6,5},{7,0},{8,15},{9,10},{10,... | collective-permute-start | bytes 307208 | tf_op jit(solution)/shard_map/ppermute | solution.py:40
  18.6 4.3 %collective-permute-start.7 = (bf16[400,128]{1,0:T(8,128)(2,1)S(1)}, bf16[400,128]{1,0:T(8,128)(2,1)S(1)}, u32[]{:S(2)}, u32[]{:S(2)}) collective-permute-start(bf16[400,128]{1,0:T(8,128)(2,1)S(1)} %get-tuple-element.60), channel_id=1, source_target_pairs={{0,1},{1,0},{2,3},{3,2},{4,5},{5,4},{6,7},{7,6},{8,9},{9,8},{10,11... | collective-permute-start | bytes 307208 | tf_op jit(solution)/shard_map/ppermute | solution.py:40
  26.6 7.4 %collective-permute-start.8 = (bf16[400,128]{1,0:T(8,128)(2,1)S(1)}, bf16[400,128]{1,0:T(8,128)(2,1)S(1)}, u32[]{:S(2)}, u32[]{:S(2)}) collective-permute-start(bf16[400,128]{1,0:T(8,128)(2,1)S(1)} %get-tuple-element.82), channel_id=1, source_target_pairs={{0,8},{1,9},{2,10},{3,11},{4,12},{5,13},{6,14},{7,15},{8,0},{9,1},... | collective-permute-start | bytes 307208 | tf_op jit(solution)/shard_map/ppermute | solution.py:40
  26.7 8.7 %collective-permute-start.9 = (bf16[400,128]{1,0:T(8,128)(2,1)S(1)}, bf16[400,128]{1,0:T(8,128)(2,1)S(1)}, u32[]{:S(2)}, u32[]{:S(2)}) collective-permute-start(bf16[400,128]{1,0:T(8,128)(2,1)S(1)} %get-tuple-element.83), channel_id=1, source_target_pairs={{0,24},{1,25},{2,26},{3,27},{4,28},{5,29},{6,30},{7,31},{8,16},{9,... | collective-permute-start | bytes 307208 | tf_op jit(solution)/shard_map/ppermute | solution.py:40
  26.8 15.6 %collective-permute-start.10 = (bf16[400,128]{1,0:T(8,128)(2,1)S(1)}, bf16[400,128]{1,0:T(8,128)(2,1)S(1)}, u32[]{:S(2)}, u32[]{:S(2)}) collective-permute-start(bf16[400,128]{1,0:T(8,128)(2,1)S(1)} %get-tuple-element.84), channel_id=1, source_target_pairs={{0,31},{1,26},{2,25},{3,28},{4,27},{5,30},{6,29},{7,24},{8,23},{9,... | collective-permute-start | bytes 307208 | tf_op jit(solution)/shard_map/ppermute | solution.py:40
  30.6 15.9 %collective-permute-start.11 = (bf16[400,128]{1,0:T(8,128)(2,1)S(1)}, bf16[400,128]{1,0:T(8,128)(2,1)S(1)}, u32[]{:S(2)}, u32[]{:S(2)}) collective-permute-start(bf16[400,128]{1,0:T(8,128)(2,1)S(1)} %get-tuple-element.85), channel_id=1, source_target_pairs={{0,15},{1,10},{2,9},{3,12},{4,11},{5,14},{6,13},{7,8},{8,7},{9,2},... | collective-permute-start | bytes 307208 | tf_op jit(solution)/shard_map/ppermute | solution.py:40
  34.0 12.4 %collective-permute-start.12 = (bf16[400,128]{1,0:T(8,128)(2,1)S(1)}, bf16[400,128]{1,0:T(8,128)(2,1)S(1)}, u32[]{:S(2)}, u32[]{:S(2)}) collective-permute-start(bf16[400,128]{1,0:T(8,128)(2,1)S(1)} %get-tuple-element.86), channel_id=1, source_target_pairs={{0,25},{1,24},{2,27},{3,26},{4,29},{5,28},{6,31},{7,30},{8,17},{9,... | collective-permute-start | bytes 307208 | tf_op jit(solution)/shard_map/ppermute | solution.py:40
  34.0 12.4 %collective-permute-start.13 = (bf16[400,128]{1,0:T(8,128)(2,1)S(1)}, bf16[400,128]{1,0:T(8,128)(2,1)S(1)}, u32[]{:S(2)}, u32[]{:S(2)}) collective-permute-start(bf16[400,128]{1,0:T(8,128)(2,1)S(1)} %get-tuple-element.87), channel_id=1, source_target_pairs={{0,9},{1,8},{2,11},{3,10},{4,13},{5,12},{6,15},{7,14},{8,1},{9,0},... | collective-permute-start | bytes 307208 | tf_op jit(solution)/shard_map/ppermute | solution.py:40
  35.4 11.0 %collective-permute-start.14 = (bf16[400,128]{1,0:T(8,128)(2,1)S(1)}, bf16[400,128]{1,0:T(8,128)(2,1)S(1)}, u32[]{:S(2)}, u32[]{:S(2)}) collective-permute-start(bf16[400,128]{1,0:T(8,128)(2,1)S(1)} %get-tuple-element.88), channel_id=1, source_target_pairs={{0,7},{1,2},{2,1},{3,4},{4,3},{5,6},{6,5},{7,0},{8,15},{9,10},{10,... | collective-permute-start | bytes 307208 | tf_op jit(solution)/shard_map/ppermute | solution.py:40
  42.3 4.1 %collective-permute-start.15 = (bf16[400,128]{1,0:T(8,128)(2,1)S(1)}, bf16[400,128]{1,0:T(8,128)(2,1)S(1)}, u32[]{:S(2)}, u32[]{:S(2)}) collective-permute-start(bf16[400,128]{1,0:T(8,128)(2,1)S(1)} %get-tuple-element.89), channel_id=1, source_target_pairs={{0,1},{1,0},{2,3},{3,2},{4,5},{5,4},{6,7},{7,6},{8,9},{9,8},{10,11... | collective-permute-start | bytes 307208 | tf_op jit(solution)/shard_map/ppermute | solution.py:40

commit v3 on v2

--- a/solution.py
+++ b/solution.py
@@ -13,14 +13,23 @@
 SWAPS = ((0, None), (1, None), (1, 1), (0, 1), (1, 0), (0, 0), (None, 1), (None, 0))
 
 
-def step_of(axis, parity):
-    if parity is None:
-        return 0
-    return jnp.where(lax.rem(lax.axis_index(axis), 2) == parity, 1, -1)
+def parity_along_gx(swap, y, ny):
+    if swap[1] is None:
+        kind = lax.rem(y, 2)
+    else:
+        kind = lax.rem(lax.div(lax.rem(y + swap[1], ny), 2), 2)
+    return lax.rem(swap[0] + kind, 2)
+
+
+def step_of(place, parity):
+    return jnp.where(lax.rem(place, 2) == parity, 1, -1)
 
 
 def received_direction(swap):
-    place = 3 * (step_of("gx", swap[0]) + 1) + step_of("gy", swap[1]) + 1
+    x, y = lax.axis_index("gx"), lax.axis_index("gy")
+    dx = 0 if swap[0] is None else step_of(x, parity_along_gx(swap, y, lax.axis_size("gy")))
+    dy = 0 if swap[1] is None else step_of(y, swap[1])
+    place = 3 * (dx + 1) + dy + 1
     return place - jnp.where(place > 4, 1, 0)
 
 
@@ -32,8 +41,14 @@
             return place
         return (place + (1 if place % 2 == parity else -1)) % size
 
+    def parity_x(y):
+        if swap[0] is None:
+            return None
+        kind = y % 2 if swap[1] is None else (y + swap[1]) % ny // 2 % 2
+        return (swap[0] + kind) % 2
+
     pairs = [
-        (x * ny + y, partner(x, nx, swap[0]) * ny + partner(y, ny, swap[1]))
+        (x * ny + y, partner(x, nx, parity_x(y)) * ny + partner(y, ny, swap[1]))
         for x in range(nx)
         for y in range(ny)
     ]

time: 47.9 us -> 44.9 us (0.937)
  the two profiles are of different devices: /device:TPU:19 before, /device:TPU:0 now
where the time goes in v3:
time: 44.9 us; the launch traced here: 44.6 us
  starting transfers between devices  27.7 us (62%)
  Pallas kernels  15.4 us (34%)
  waiting for transfers between devices  0.79 us (2%)
  between operations  0.73 us (2%)
    ppermute x16, starting transfers between devices, traded(): return lax.ppermute(value, ('gx', 'gy'), pairs)  27.7 us
    pallas_call x7, Pallas kernels, run(): pl.pallas_call(kernel, out_shape=outs, in_specs=[HB if n in far else VM f...  15.4 us
  transfers between devices with their start and end apart: 16, of which 1 were waited for; matrix products, arithmetic and copies ran while one was open for 0% of the time, Pallas kernels for 20%

profile of v3, /device:TPU:0, one launch (start us, length us, event | category | flops | bytes accessed | tf_op | source)
XLA Modules:
  0.0 44.6 jit_solution(11288711186094006852)
XLA Ops:
  0.6 1.4 %shard_map.140 = (bf16[400,128]{1,0:T(8,128)(2,1)S(1)}, bf16[400,128]{1,0:T(8,128)(2,1)S(1)}, bf16[400,128]{1,0:T(8,128)(2,1)S(1)}, bf16[400,128]{1,0:T(8,128)(2...) custom-call(bf16[1600,128]{1,0:T(8,128)(2,1)} %bitcast.12, s32[8,32]{1,0:T(8,128)} %bitcast.16), custom_call_target="tpu_custom_call" | custom-call | tf_op jit(solution)/shard_map/pallas_call | solution.py:393
  2.0 3.1 %collective-permute-start = (bf16[400,128]{1,0:T(8,128)(2,1)S(1)}, bf16[400,128]{1,0:T(8,128)(2,1)S(1)}, u32[]{:S(2)}, u32[]{:S(2)}) collective-permute-start(bf16[400,128]{1,0:T(8,128)(2,1)S(1)} %get-tuple-element.53), channel_id=1, source_target_pairs={{0,8},{1,25},{2,10},{3,27},{4,12},{5,29},{6,14},{7,31},{8,0},{9,17... | collective-permute-start | bytes 307208 | tf_op jit(solution)/shard_map/ppermute | solution.py:55
  5.2 2.5 %collective-permute-start.1 = (bf16[400,128]{1,0:T(8,128)(2,1)S(1)}, bf16[400,128]{1,0:T(8,128)(2,1)S(1)}, u32[]{:S(2)}, u32[]{:S(2)}) collective-permute-start(bf16[400,128]{1,0:T(8,128)(2,1)S(1)} %get-tuple-element.54), channel_id=1, source_target_pairs={{0,24},{1,9},{2,26},{3,11},{4,28},{5,13},{6,30},{7,15},{8,16},{9,1... | collective-permute-start | bytes 307208 | tf_op jit(solution)/shard_map/ppermute | solution.py:55
  7.6 1.2 %collective-permute-start.2 = (bf16[400,128]{1,0:T(8,128)(2,1)S(1)}, bf16[400,128]{1,0:T(8,128)(2,1)S(1)}, u32[]{:S(2)}, u32[]{:S(2)}) collective-permute-start(bf16[400,128]{1,0:T(8,128)(2,1)S(1)} %get-tuple-element.55), channel_id=1, source_target_pairs={{0,31},{1,10},{2,9},{3,28},{4,27},{5,14},{6,13},{7,24},{8,23},{9,2... | collective-permute-start | bytes 307208 | tf_op jit(solution)/shard_map/ppermute | solution.py:55
  8.8 1.1 %collective-permute-start.3 = (bf16[400,128]{1,0:T(8,128)(2,1)S(1)}, bf16[400,128]{1,0:T(8,128)(2,1)S(1)}, u32[]{:S(2)}, u32[]{:S(2)}) collective-permute-start(bf16[400,128]{1,0:T(8,128)(2,1)S(1)} %get-tuple-element.56), channel_id=1, source_target_pairs={{0,15},{1,26},{2,25},{3,12},{4,11},{5,30},{6,29},{7,8},{8,7},{9,18... | collective-permute-start | bytes 307208 | tf_op jit(solution)/shard_map/ppermute | solution.py:55
  10.0 0.4 %shard_map.142 = (bf16[400,128]{1,0:T(8,128)(2,1)S(1)}, bf16[400,128]{1,0:T(8,128)(2,1)S(1)}, bf16[400,128]{1,0:T(8,128)(2,1)S(1)}, bf16[400,128]{1,0:T(8,128)(2,1)S(1)}) custom-call(bf16[1600,128]{1,0:T(8,128)(2,1)S(1)} %get-tuple-element.47.own_ref.refs_0_, s32[8,32]{1,0:T(8,128)S(1)} %get-tuple-element.50.lists_ref.refs_3_), custom_call_target="tpu_custom_call" | custom-call | tf_op jit(solution)/shard_map/pallas_call | solution.py:393
  10.4 2.6 %collective-permute-start.4 = (bf16[400,128]{1,0:T(8,128)(2,1)S(1)}, bf16[400,128]{1,0:T(8,128)(2,1)S(1)}, u32[]{:S(2)}, u32[]{:S(2)}) collective-permute-start(bf16[400,128]{1,0:T(8,128)(2,1)S(1)} %get-tuple-element.57), channel_id=1, source_target_pairs={{0,25},{1,24},{2,11},{3,10},{4,29},{5,28},{6,15},{7,14},{8,17},{9,... | collective-permute-start | bytes 307208 | tf_op jit(solution)/shard_map/ppermute | solution.py:55
  13.1 0.0 collective-permute-done.refs_0_
  13.1 1.3 %collective-permute-start.5 = (bf16[400,128]{1,0:T(8,128)(2,1)S(1)}, bf16[400,128]{1,0:T(8,128)(2,1)S(1)}, u32[]{:S(2)}, u32[]{:S(2)}) collective-permute-start(bf16[400,128]{1,0:T(8,128)(2,1)S(1)} %get-tuple-element.58), channel_id=1, source_target_pairs={{0,9},{1,8},{2,27},{3,26},{4,13},{5,12},{6,31},{7,30},{8,1},{9,0},... | collective-permute-start | bytes 307208 | tf_op jit(solution)/shard_map/ppermute | solution.py:55
  14.3 0.0 collective-permute-done.1.refs_1_
  14.3 2.1 %collective-permute-start.6 = (bf16[400,128]{1,0:T(8,128)(2,1)S(1)}, bf16[400,128]{1,0:T(8,128)(2,1)S(1)}, u32[]{:S(2)}, u32[]{:S(2)}) collective-permute-start(bf16[400,128]{1,0:T(8,128)(2,1)S(1)} %get-tuple-element.59), channel_id=1, source_target_pairs={{0,7},{1,2},{2,1},{3,4},{4,3},{5,6},{6,5},{7,0},{8,15},{9,10},{10,... | collective-permute-start | bytes 307208 | tf_op jit(solution)/shard_map/ppermute | solution.py:55
  16.4 0.0 collective-permute-done.2.refs_2_
  16.4 0.0 collective-permute-start.7
  16.4 4.2 %shard_map.141 = (f32[4,832,256]{2,1,0:T(8,128)S(1)}, f32[4,832,256]{2,1,0:T(8,128)S(1)}, f32[4,832,256]{2,1,0:T(8,128)S(1)}, bf16[4,200,200]{2,1,0:T(8,128)(2,1...) custom-call(bf16[1600,128]{1,0:T(8,128)(2,1)S(1)} %get-tuple-element, ...), custom_call_target="tpu_custom_call" | custom-call | tf_op jit(solution)/shard_map/pallas_call | solution.py:393
  20.6 0.0 collective-permute-done.3.refs_3_
  20.6 0.0 collective-permute-done.4.refs_4_
  20.6 0.0 collective-permute-done.5.refs_5_
  20.6 0.0 collective-permute-done.6.refs_6_
  20.7 0.0 collective-permute-done.7.refs_7_
  20.7 3.7 %shard_map.143 = (bf16[400,128]{1,0:T(8,128)(2,1)S(1)}, bf16[400,128]{1,0:T(8,128)(2,1)S(1)}, bf16[400,128]{1,0:T(8,128)(2,1)S(1)}, bf16[400,128]{1,0:T(8,128)(2...) custom-call(bf16[400,128]{1,0:T(8,128)(2,1)S(1)} %collective-permute-done.refs_0_, ...), custom_call_target="tpu_custom_call" | custom-call | tf_op jit(solution)/shard_map/pallas_call | solution.py:393
  24.4 2.3 %collective-permute-start.8 = (bf16[400,128]{1,0:T(8,128)(2,1)S(1)}, bf16[400,128]{1,0:T(8,128)(2,1)S(1)}, u32[]{:S(2)}, u32[]{:S(2)}) collective-permute-start(bf16[400,128]{1,0:T(8,128)(2,1)S(1)} %get-tuple-element.82), channel_id=1, source_target_pairs={{0,8},{1,25},{2,10},{3,27},{4,12},{5,29},{6,14},{7,31},{8,0},{9,17... | collective-permute-start | bytes 307208 | tf_op jit(solution)/shard_map/ppermute | solution.py:55
  26.6 1.6 %collective-permute-start.9 = (bf16[400,128]{1,0:T(8,128)(2,1)S(1)}, bf16[400,128]{1,0:T(8,128)(2,1)S(1)}, u32[]{:S(2)}, u32[]{:S(2)}) collective-permute-start(bf16[400,128]{1,0:T(8,128)(2,1)S(1)} %get-tuple-element.83), channel_id=1, source_target_pairs={{0,24},{1,9},{2,26},{3,11},{4,28},{5,13},{6,30},{7,15},{8,16},{9,1... | collective-permute-start | bytes 307208 | tf_op jit(solution)/shard_map/ppermute | solution.py:55
  28.2 3.6 %collective-permute-start.10 = (bf16[400,128]{1,0:T(8,128)(2,1)S(1)}, bf16[400,128]{1,0:T(8,128)(2,1)S(1)}, u32[]{:S(2)}, u32[]{:S(2)}) collective-permute-start(bf16[400,128]{1,0:T(8,128)(2,1)S(1)} %get-tuple-element.84), channel_id=1, source_target_pairs={{0,31},{1,10},{2,9},{3,28},{4,27},{5,14},{6,13},{7,24},{8,23},{9,2... | collective-permute-start | bytes 307208 | tf_op jit(solution)/shard_map/ppermute | solution.py:55
  31.8 0.4 shard_map.145
  32.3 0.1 collective-permute-start.11
  32.3 3.8 %collective-permute-start.12 = (bf16[400,128]{1,0:T(8,128)(2,1)S(1)}, bf16[400,128]{1,0:T(8,128)(2,1)S(1)}, u32[]{:S(2)}, u32[]{:S(2)}) collective-permute-start(bf16[400,128]{1,0:T(8,128)(2,1)S(1)} %get-tuple-element.86), channel_id=1, source_target_pairs={{0,25},{1,24},{2,11},{3,10},{4,29},{5,28},{6,15},{7,14},{8,17},{9,... | collective-permute-start | bytes 307208 | tf_op jit(solution)/shard_map/ppermute | solution.py:55
  36.1 0.0 collective-permute-done.8.refs_0_
  36.1 0.0 collective-permute-start.13
  36.1 0.0 collective-permute-done.9.refs_1_
  36.1 2.2 %collective-permute-start.14 = (bf16[400,128]{1,0:T(8,128)(2,1)S(1)}, bf16[400,128]{1,0:T(8,128)(2,1)S(1)}, u32[]{:S(2)}, u32[]{:S(2)}) collective-permute-start(bf16[400,128]{1,0:T(8,128)(2,1)S(1)} %get-tuple-element.88), channel_id=1, source_target_pairs={{0,7},{1,2},{2,1},{3,4},{4,3},{5,6},{6,5},{7,0},{8,15},{9,10},{10,... | collective-permute-start | bytes 307208 | tf_op jit(solution)/shard_map/ppermute | solution.py:55
  38.3 0.0 collective-permute-done.10.refs_2_
  38.4 0.2 collective-permute-start.15
  38.6 4.1 %shard_map.144 = (bf16[25,4,16,128]{3,2,1,0:T(8,128)(2,1)}, f32[25,8,8,128]{3,2,1,0:T(8,128)S(1)}, bf16[4,128,256]{2,1,0:T(8,128)(2,1)S(1)}) custom-call(bf16[1600,128]{1,0:T(8,128)(2,1)S(1)} %get-tuple-element.47.own_ref.refs_0_, bf16[1600,128]{1,0:T(8,128)(2,1)S(1)} %get-tuple-element.48.refs_1_, s32[1,256]{1,0:T(1,128)S(1)} %get-tuple-element.49.refs_2_, ...), custom_call_target="tpu_custom_call" | custom-call | tf_op jit(solution)/shard_map/pallas_call | solution.py:393
  42.6 0.0 collective-permute-done.11.refs_3_
  42.6 0.0 collective-permute-done.12.refs_4_
  42.6 0.7 %collective-permute-done.13.refs_5_ = bf16[400,128]{1,0:T(8,128)(2,1)S(1)} collective-permute-done((bf16[400,128]{1,0:T(8,128)(2,1)S(1)}, bf16[400,128]{1,0:T(8,128)(2,1)S(1)}, u32[]{:S(2)}, u32[]{:S(2)}) %collective-permute-start.13) | collective-permute-done | bytes 102432 | tf_op jit(solution)/shard_map/ppermute | solution.py:55
  43.4 0.0 collective-permute-done.14.refs_6_
  43.4 0.0 collective-permute-done.15.refs_7_
  43.4 1.2 %shard_map.146 = f32[25,64,128]{2,1,0:T(8,128)} custom-call(bf16[400,128]{1,0:T(8,128)(2,1)S(1)} %collective-permute-done.8.refs_0_, bf16[400,128]{1,0:T(8,128)(2,1)S(1)} %collective-permute-done.9.refs_1_, bf16[400,128]{1,0:T(8,128)(2,1)S(1)} %collective-permute-done.10.refs_2_, bf16[400,128]{1,0:T(8,128)(2,1)S(1)} %collective-permute-done.11.refs_3_, ...), custom_call_target="tpu_custom_call" | custom-call | tf_op jit(solution)/shard_map/pallas_call | solution.py:393
Async XLA Ops:
  2.0 11.0 %collective-permute-start = (bf16[400,128]{1,0:T(8,128)(2,1)S(1)}, bf16[400,128]{1,0:T(8,128)(2,1)S(1)}, u32[]{:S(2)}, u32[]{:S(2)}) collective-permute-start(bf16[400,128]{1,0:T(8,128)(2,1)S(1)} %get-tuple-element.53), channel_id=1, source_target_pairs={{0,8},{1,25},{2,10},{3,27},{4,12},{5,29},{6,14},{7,31},{8,0},{9,17... | collective-permute-start | bytes 307208 | tf_op jit(solution)/shard_map/ppermute | solution.py:55
  5.2 9.2 %collective-permute-start.1 = (bf16[400,128]{1,0:T(8,128)(2,1)S(1)}, bf16[400,128]{1,0:T(8,128)(2,1)S(1)}, u32[]{:S(2)}, u32[]{:S(2)}) collective-permute-start(bf16[400,128]{1,0:T(8,128)(2,1)S(1)} %get-tuple-element.54), channel_id=1, source_target_pairs={{0,24},{1,9},{2,26},{3,11},{4,28},{5,13},{6,30},{7,15},{8,16},{9,1... | collective-permute-start | bytes 307208 | tf_op jit(solution)/shard_map/ppermute | solution.py:55
  7.6 8.8 %collective-permute-start.2 = (bf16[400,128]{1,0:T(8,128)(2,1)S(1)}, bf16[400,128]{1,0:T(8,128)(2,1)S(1)}, u32[]{:S(2)}, u32[]{:S(2)}) collective-permute-start(bf16[400,128]{1,0:T(8,128)(2,1)S(1)} %get-tuple-element.55), channel_id=1, source_target_pairs={{0,31},{1,10},{2,9},{3,28},{4,27},{5,14},{6,13},{7,24},{8,23},{9,2... | collective-permute-start | bytes 307208 | tf_op jit(solution)/shard_map/ppermute | solution.py:55
  8.8 11.8 %collective-permute-start.3 = (bf16[400,128]{1,0:T(8,128)(2,1)S(1)}, bf16[400,128]{1,0:T(8,128)(2,1)S(1)}, u32[]{:S(2)}, u32[]{:S(2)}) collective-permute-start(bf16[400,128]{1,0:T(8,128)(2,1)S(1)} %get-tuple-element.56), channel_id=1, source_target_pairs={{0,15},{1,26},{2,25},{3,12},{4,11},{5,30},{6,29},{7,8},{8,7},{9,18... | collective-permute-start | bytes 307208 | tf_op jit(solution)/shard_map/ppermute | solution.py:55
  10.4 10.2 %collective-permute-start.4 = (bf16[400,128]{1,0:T(8,128)(2,1)S(1)}, bf16[400,128]{1,0:T(8,128)(2,1)S(1)}, u32[]{:S(2)}, u32[]{:S(2)}) collective-permute-start(bf16[400,128]{1,0:T(8,128)(2,1)S(1)} %get-tuple-element.57), channel_id=1, source_target_pairs={{0,25},{1,24},{2,11},{3,10},{4,29},{5,28},{6,15},{7,14},{8,17},{9,... | collective-permute-start | bytes 307208 | tf_op jit(solution)/shard_map/ppermute | solution.py:55
  13.1 7.6 %collective-permute-start.5 = (bf16[400,128]{1,0:T(8,128)(2,1)S(1)}, bf16[400,128]{1,0:T(8,128)(2,1)S(1)}, u32[]{:S(2)}, u32[]{:S(2)}) collective-permute-start(bf16[400,128]{1,0:T(8,128)(2,1)S(1)} %get-tuple-element.58), channel_id=1, source_target_pairs={{0,9},{1,8},{2,27},{3,26},{4,13},{5,12},{6,31},{7,30},{8,1},{9,0},... | collective-permute-start | bytes 307208 | tf_op jit(solution)/shard_map/ppermute | solution.py:55
  14.3 6.3 %collective-permute-start.6 = (bf16[400,128]{1,0:T(8,128)(2,1)S(1)}, bf16[400,128]{1,0:T(8,128)(2,1)S(1)}, u32[]{:S(2)}, u32[]{:S(2)}) collective-permute-start(bf16[400,128]{1,0:T(8,128)(2,1)S(1)} %get-tuple-element.59), channel_id=1, source_target_pairs={{0,7},{1,2},{2,1},{3,4},{4,3},{5,6},{6,5},{7,0},{8,15},{9,10},{10,... | collective-permute-start | bytes 307208 | tf_op jit(solution)/shard_map/ppermute | solution.py:55
  16.4 4.2 %collective-permute-start.7 = (bf16[400,128]{1,0:T(8,128)(2,1)S(1)}, bf16[400,128]{1,0:T(8,128)(2,1)S(1)}, u32[]{:S(2)}, u32[]{:S(2)}) collective-permute-start(bf16[400,128]{1,0:T(8,128)(2,1)S(1)} %get-tuple-element.60), channel_id=1, source_target_pairs={{0,1},{1,0},{2,3},{3,2},{4,5},{5,4},{6,7},{7,6},{8,9},{9,8},{10,11... | collective-permute-start | bytes 307208 | tf_op jit(solution)/shard_map/ppermute | solution.py:55
  24.4 11.8 %collective-permute-start.8 = (bf16[400,128]{1,0:T(8,128)(2,1)S(1)}, bf16[400,128]{1,0:T(8,128)(2,1)S(1)}, u32[]{:S(2)}, u32[]{:S(2)}) collective-permute-start(bf16[400,128]{1,0:T(8,128)(2,1)S(1)} %get-tuple-element.82), channel_id=1, source_target_pairs={{0,8},{1,25},{2,10},{3,27},{4,12},{5,29},{6,14},{7,31},{8,0},{9,17... | collective-permute-start | bytes 307208 | tf_op jit(solution)/shard_map/ppermute | solution.py:55
  26.6 9.5 %collective-permute-start.9 = (bf16[400,128]{1,0:T(8,128)(2,1)S(1)}, bf16[400,128]{1,0:T(8,128)(2,1)S(1)}, u32[]{:S(2)}, u32[]{:S(2)}) collective-permute-start(bf16[400,128]{1,0:T(8,128)(2,1)S(1)} %get-tuple-element.83), channel_id=1, source_target_pairs={{0,24},{1,9},{2,26},{3,11},{4,28},{5,13},{6,30},{7,15},{8,16},{9,1... | collective-permute-start | bytes 307208 | tf_op jit(solution)/shard_map/ppermute | solution.py:55
  28.2 10.2 %collective-permute-start.10 = (bf16[400,128]{1,0:T(8,128)(2,1)S(1)}, bf16[400,128]{1,0:T(8,128)(2,1)S(1)}, u32[]{:S(2)}, u32[]{:S(2)}) collective-permute-start(bf16[400,128]{1,0:T(8,128)(2,1)S(1)} %get-tuple-element.84), channel_id=1, source_target_pairs={{0,31},{1,10},{2,9},{3,28},{4,27},{5,14},{6,13},{7,24},{8,23},{9,2... | collective-permute-start | bytes 307208 | tf_op jit(solution)/shard_map/ppermute | solution.py:55
  32.3 10.4 %collective-permute-start.11 = (bf16[400,128]{1,0:T(8,128)(2,1)S(1)}, bf16[400,128]{1,0:T(8,128)(2,1)S(1)}, u32[]{:S(2)}, u32[]{:S(2)}) collective-permute-start(bf16[400,128]{1,0:T(8,128)(2,1)S(1)} %get-tuple-element.85), channel_id=1, source_target_pairs={{0,15},{1,26},{2,25},{3,12},{4,11},{5,30},{6,29},{7,8},{8,7},{9,18... | collective-permute-start | bytes 307208 | tf_op jit(solution)/shard_map/ppermute | solution.py:55
  32.3 10.3 %collective-permute-start.12 = (bf16[400,128]{1,0:T(8,128)(2,1)S(1)}, bf16[400,128]{1,0:T(8,128)(2,1)S(1)}, u32[]{:S(2)}, u32[]{:S(2)}) collective-permute-start(bf16[400,128]{1,0:T(8,128)(2,1)S(1)} %get-tuple-element.86), channel_id=1, source_target_pairs={{0,25},{1,24},{2,11},{3,10},{4,29},{5,28},{6,15},{7,14},{8,17},{9,... | collective-permute-start | bytes 307208 | tf_op jit(solution)/shard_map/ppermute | solution.py:55
  36.1 7.2 %collective-permute-start.13 = (bf16[400,128]{1,0:T(8,128)(2,1)S(1)}, bf16[400,128]{1,0:T(8,128)(2,1)S(1)}, u32[]{:S(2)}, u32[]{:S(2)}) collective-permute-start(bf16[400,128]{1,0:T(8,128)(2,1)S(1)} %get-tuple-element.87), channel_id=1, source_target_pairs={{0,9},{1,8},{2,27},{3,26},{4,13},{5,12},{6,31},{7,30},{8,1},{9,0},... | collective-permute-start | bytes 307208 | tf_op jit(solution)/shard_map/ppermute | solution.py:55
  36.1 7.2 %collective-permute-start.14 = (bf16[400,128]{1,0:T(8,128)(2,1)S(1)}, bf16[400,128]{1,0:T(8,128)(2,1)S(1)}, u32[]{:S(2)}, u32[]{:S(2)}) collective-permute-start(bf16[400,128]{1,0:T(8,128)(2,1)S(1)} %get-tuple-element.88), channel_id=1, source_target_pairs={{0,7},{1,2},{2,1},{3,4},{4,3},{5,6},{6,5},{7,0},{8,15},{9,10},{10,... | collective-permute-start | bytes 307208 | tf_op jit(solution)/shard_map/ppermute | solution.py:55
  38.4 5.0 %collective-permute-start.15 = (bf16[400,128]{1,0:T(8,128)(2,1)S(1)}, bf16[400,128]{1,0:T(8,128)(2,1)S(1)}, u32[]{:S(2)}, u32[]{:S(2)}) collective-permute-start(bf16[400,128]{1,0:T(8,128)(2,1)S(1)} %get-tuple-element.89), channel_id=1, source_target_pairs={{0,1},{1,0},{2,3},{3,2},{4,5},{5,4},{6,7},{7,6},{8,9},{9,8},{10,11... | collective-permute-start | bytes 307208 | tf_op jit(solution)/shard_map/ppermute | solution.py:55

commit v4 on v3

--- a/solution.py
+++ b/solution.py
@@ -179,9 +179,9 @@
 
 def local_kernel(own_ref, *refs):
     given, refs = refs[:11], refs[11:]
-    feat_ref, prod_ref, gate_ref, up_ref, down_ref, fdown_ref, part_ref, picks_ref, both_ref = refs[:9]
+    feat_ref, prod_ref, gate_ref, up_ref, down_ref, from_ref, part_ref, picks_ref, both_ref = refs[:9]
     turned, kept, refs = refs[9:14], refs[14:23], refs[23:]
-    to_ref, from_ref, fup, filt, sems = refs
+    to_ref, fup, filt, sems = refs
     copies = fetch(given, (to_ref, from_ref, *kept), sems)
     cot_ref, weights, harm_ref, src_ref, tgt_ref = kept[0], kept[1:6], kept[6], kept[7], kept[8]
     rows, atoms = own_ref.shape
@@ -196,7 +196,6 @@
         fup[s] = up_matrices(from_parts, s)
     for n in range(2):
         down_ref[n] = down_matrix(to_parts[n], padded)
-        fdown_ref[n] = down_matrix(from_parts[n], padded)
     for copy in copies[2:]:
         copy.wait()
     own = own_ref[...].astype(F32)
@@ -333,8 +332,8 @@
 
 
 def after_kernel(*refs):
-    own_ref, cot_ref, src_ref, lists_ref, down_ref, fdown_ref = refs[:6]
-    act_ref, feat_ref, prod_ref, dsrc_ref, out_ref, grad_ref, lent_ref = refs[6:]
+    own_ref, cot_ref, src_ref, lists_ref, down_ref, from_ref = refs[:6]
+    act_ref, feat_ref, prod_ref, dsrc_ref, out_ref, grad_ref, lent_ref, fdown_ref = refs[6:]
     rows, atoms = own_ref.shape
     channels = rows // COEFS
     edges = src_ref.shape[1]
@@ -346,6 +345,9 @@
         lists = lent_lists(lists_ref, SWAPS[4 * g : 4 * g + 4])
         for q in range(4):
             lent_ref[q, :, g * atoms : (g + 1) * atoms] = lent_pick(lists, q)
+
+    for n, part in enumerate(split(from_ref[...])):
+        fdown_ref[n] = down_matrix(part, fdown_ref.shape[2] // 4)
 
     def down(parts, value):
         high, low = split(value)
@@ -445,7 +447,7 @@
     )
     given = (to_grid.T, from_grid, *kept)
     downs = like((2, 8 * COEFS, 4 * padded), BF16)
-    feat, prod, gate, up, down, fdown, part, picks, both, *near = call(
+    feat, prod, gate, up, down, from_near, part, picks, both, *near = call(
         local_kernel,
         [
             grid,
@@ -453,7 +455,7 @@
             grid,
             like((4, 2 * points, 8 * COEFS), BF16),
             downs,
-            downs,
+            same(from_grid),
             like((rows, atoms), F32),
             like((4, 2 * atoms, edges), BF16),
             like((2 * atoms, edges), BF16),
@@ -461,7 +463,6 @@
             *map(same, kept),
         ],
         [
-            pltpu.VMEM((COEFS, points), F32),
             pltpu.VMEM((COEFS, points), F32),
             pltpu.VMEM((4, 2 * points, 8 * COEFS), BF16),
             pltpu.VMEM((COEFS, channels, edges), BF16),
@@ -491,7 +492,8 @@
             like((COEFS, channels // 8, 8, atoms), F32),
             like((4, atoms, 2 * atoms), BF16),
         ],
-    )(own, cot, src, lists, down, fdown, act, feat, prod, dsrc)
+        [pltpu.VMEM(downs.shape, BF16)],
+    )(own, cot, src, lists, down, from_near, act, feat, prod, dsrc)
     total = call(
         final_kernel,
         pltpu.HBM((COEFS, channels, atoms), F32),

time: 44.9 us -> 44.4 us (0.989)
  starting transfers between devices: 27.7 us -> 27.2 us
  transfers between devices with their start and end apart: 16 -> 16, of which waited for: 1 -> 3; matrix products, arithmetic and copies ran while one was open for 0% -> 0% of each run, Pallas kernels for 20% -> 20%
where the time goes in v4:
time: 44.4 us; the launch traced here: 44.1 us
  starting transfers between devices  27.2 us (61%)
  Pallas kernels  15.2 us (34%)
  waiting for transfers between devices  0.96 us (2%)
  between operations  0.71 us (2%)
    ppermute x16, starting transfers between devices, traded(): return lax.ppermute(value, ('gx', 'gy'), pairs)  27.2 us
    pallas_call x7, Pallas kernels, run(): pl.pallas_call(kernel, out_shape=outs, in_specs=[HB if n in far else VM f...  15.2 us
    ppermute x16, waiting for transfers between devices, traded(): return lax.ppermute(value, ('gx', 'gy'), pairs)  0.96 us
  transfers between devices with their start and end apart: 16, of which 3 were waited for; matrix products, arithmetic and copies ran while one was open for 0% of the time, Pallas kernels for 20%

profile of v4, /device:TPU:0, one launch (start us, length us, event | category | flops | bytes accessed | tf_op | source)
XLA Modules:
  0.0 44.1 jit_solution(10330676879008350196)
XLA Ops:
  0.6 1.4 %shard_map.140 = (bf16[400,128]{1,0:T(8,128)(2,1)S(1)}, bf16[400,128]{1,0:T(8,128)(2,1)S(1)}, bf16[400,128]{1,0:T(8,128)(2,1)S(1)}, bf16[400,128]{1,0:T(8,128)(2...) custom-call(bf16[1600,128]{1,0:T(8,128)(2,1)} %bitcast.12, s32[8,32]{1,0:T(8,128)} %bitcast.16), custom_call_target="tpu_custom_call" | custom-call | tf_op jit(solution)/shard_map/pallas_call | solution.py:395
  2.0 3.1 %collective-permute-start = (bf16[400,128]{1,0:T(8,128)(2,1)S(1)}, bf16[400,128]{1,0:T(8,128)(2,1)S(1)}, u32[]{:S(2)}, u32[]{:S(2)}) collective-permute-start(bf16[400,128]{1,0:T(8,128)(2,1)S(1)} %get-tuple-element.53), channel_id=1, source_target_pairs={{0,8},{1,25},{2,10},{3,27},{4,12},{5,29},{6,14},{7,31},{8,0},{9,17... | collective-permute-start | bytes 307208 | tf_op jit(solution)/shard_map/ppermute | solution.py:55
  5.2 2.5 %collective-permute-start.1 = (bf16[400,128]{1,0:T(8,128)(2,1)S(1)}, bf16[400,128]{1,0:T(8,128)(2,1)S(1)}, u32[]{:S(2)}, u32[]{:S(2)}) collective-permute-start(bf16[400,128]{1,0:T(8,128)(2,1)S(1)} %get-tuple-element.54), channel_id=1, source_target_pairs={{0,24},{1,9},{2,26},{3,11},{4,28},{5,13},{6,30},{7,15},{8,16},{9,1... | collective-permute-start | bytes 307208 | tf_op jit(solution)/shard_map/ppermute | solution.py:55
  7.6 1.2 %collective-permute-start.2 = (bf16[400,128]{1,0:T(8,128)(2,1)S(1)}, bf16[400,128]{1,0:T(8,128)(2,1)S(1)}, u32[]{:S(2)}, u32[]{:S(2)}) collective-permute-start(bf16[400,128]{1,0:T(8,128)(2,1)S(1)} %get-tuple-element.55), channel_id=1, source_target_pairs={{0,31},{1,10},{2,9},{3,28},{4,27},{5,14},{6,13},{7,24},{8,23},{9,2... | collective-permute-start | bytes 307208 | tf_op jit(solution)/shard_map/ppermute | solution.py:55
  8.8 1.1 %collective-permute-start.3 = (bf16[400,128]{1,0:T(8,128)(2,1)S(1)}, bf16[400,128]{1,0:T(8,128)(2,1)S(1)}, u32[]{:S(2)}, u32[]{:S(2)}) collective-permute-start(bf16[400,128]{1,0:T(8,128)(2,1)S(1)} %get-tuple-element.56), channel_id=1, source_target_pairs={{0,15},{1,26},{2,25},{3,12},{4,11},{5,30},{6,29},{7,8},{8,7},{9,18... | collective-permute-start | bytes 307208 | tf_op jit(solution)/shard_map/ppermute | solution.py:55
  10.0 0.4 %shard_map.142 = (bf16[400,128]{1,0:T(8,128)(2,1)S(1)}, bf16[400,128]{1,0:T(8,128)(2,1)S(1)}, bf16[400,128]{1,0:T(8,128)(2,1)S(1)}, bf16[400,128]{1,0:T(8,128)(2,1)S(1)}) custom-call(bf16[1600,128]{1,0:T(8,128)(2,1)S(1)} %get-tuple-element.47.own_ref.refs_0_, s32[8,32]{1,0:T(8,128)S(1)} %get-tuple-element.50.lists_ref.refs_3_), custom_call_target="tpu_custom_call" | custom-call | tf_op jit(solution)/shard_map/pallas_call | solution.py:395
  10.4 2.6 %collective-permute-start.4 = (bf16[400,128]{1,0:T(8,128)(2,1)S(1)}, bf16[400,128]{1,0:T(8,128)(2,1)S(1)}, u32[]{:S(2)}, u32[]{:S(2)}) collective-permute-start(bf16[400,128]{1,0:T(8,128)(2,1)S(1)} %get-tuple-element.57), channel_id=1, source_target_pairs={{0,25},{1,24},{2,11},{3,10},{4,29},{5,28},{6,15},{7,14},{8,17},{9,... | collective-permute-start | bytes 307208 | tf_op jit(solution)/shard_map/ppermute | solution.py:55
  13.1 0.0 collective-permute-done.refs_0_
  13.1 1.3 %collective-permute-start.5 = (bf16[400,128]{1,0:T(8,128)(2,1)S(1)}, bf16[400,128]{1,0:T(8,128)(2,1)S(1)}, u32[]{:S(2)}, u32[]{:S(2)}) collective-permute-start(bf16[400,128]{1,0:T(8,128)(2,1)S(1)} %get-tuple-element.58), channel_id=1, source_target_pairs={{0,9},{1,8},{2,27},{3,26},{4,13},{5,12},{6,31},{7,30},{8,1},{9,0},... | collective-permute-start | bytes 307208 | tf_op jit(solution)/shard_map/ppermute | solution.py:55
  14.3 0.0 collective-permute-done.1.refs_1_
  14.3 2.1 %collective-permute-start.6 = (bf16[400,128]{1,0:T(8,128)(2,1)S(1)}, bf16[400,128]{1,0:T(8,128)(2,1)S(1)}, u32[]{:S(2)}, u32[]{:S(2)}) collective-permute-start(bf16[400,128]{1,0:T(8,128)(2,1)S(1)} %get-tuple-element.59), channel_id=1, source_target_pairs={{0,7},{1,2},{2,1},{3,4},{4,3},{5,6},{6,5},{7,0},{8,15},{9,10},{10,... | collective-permute-start | bytes 307208 | tf_op jit(solution)/shard_map/ppermute | solution.py:55
  16.4 0.0 collective-permute-done.2.refs_2_
  16.4 0.0 collective-permute-start.7
  16.4 3.7 %shard_map.141 = (f32[4,832,256]{2,1,0:T(8,128)S(1)}, f32[4,832,256]{2,1,0:T(8,128)S(1)}, f32[4,832,256]{2,1,0:T(8,128)S(1)}, bf16[4,200,200]{2,1,0:T(8,128)(2,1...) custom-call(bf16[1600,128]{1,0:T(8,128)(2,1)S(1)} %get-tuple-element, ...), custom_call_target="tpu_custom_call" | custom-call | tf_op jit(solution)/shard_map/pallas_call | solution.py:395
  20.1 0.0 collective-permute-done.3.refs_3_
  20.1 0.0 collective-permute-done.4.refs_4_
  20.1 0.3 collective-permute-done.5.refs_5_
  20.4 0.2 collective-permute-done.6.refs_6_
  20.6 0.0 collective-permute-done.7.refs_7_
  20.6 3.7 %shard_map.143 = (bf16[400,128]{1,0:T(8,128)(2,1)S(1)}, bf16[400,128]{1,0:T(8,128)(2,1)S(1)}, bf16[400,128]{1,0:T(8,128)(2,1)S(1)}, bf16[400,128]{1,0:T(8,128)(2...) custom-call(bf16[400,128]{1,0:T(8,128)(2,1)S(1)} %collective-permute-done.refs_0_, ...), custom_call_target="tpu_custom_call" | custom-call | tf_op jit(solution)/shard_map/pallas_call | solution.py:395
  24.3 1.8 %collective-permute-start.8 = (bf16[400,128]{1,0:T(8,128)(2,1)S(1)}, bf16[400,128]{1,0:T(8,128)(2,1)S(1)}, u32[]{:S(2)}, u32[]{:S(2)}) collective-permute-start(bf16[400,128]{1,0:T(8,128)(2,1)S(1)} %get-tuple-element.82), channel_id=1, source_target_pairs={{0,8},{1,25},{2,10},{3,27},{4,12},{5,29},{6,14},{7,31},{8,0},{9,17... | collective-permute-start | bytes 307208 | tf_op jit(solution)/shard_map/ppermute | solution.py:55
  26.1 1.6 %collective-permute-start.9 = (bf16[400,128]{1,0:T(8,128)(2,1)S(1)}, bf16[400,128]{1,0:T(8,128)(2,1)S(1)}, u32[]{:S(2)}, u32[]{:S(2)}) collective-permute-start(bf16[400,128]{1,0:T(8,128)(2,1)S(1)} %get-tuple-element.83), channel_id=1, source_target_pairs={{0,24},{1,9},{2,26},{3,11},{4,28},{5,13},{6,30},{7,15},{8,16},{9,1... | collective-permute-start | bytes 307208 | tf_op jit(solution)/shard_map/ppermute | solution.py:55
  27.7 3.6 %collective-permute-start.10 = (bf16[400,128]{1,0:T(8,128)(2,1)S(1)}, bf16[400,128]{1,0:T(8,128)(2,1)S(1)}, u32[]{:S(2)}, u32[]{:S(2)}) collective-permute-start(bf16[400,128]{1,0:T(8,128)(2,1)S(1)} %get-tuple-element.84), channel_id=1, source_target_pairs={{0,31},{1,10},{2,9},{3,28},{4,27},{5,14},{6,13},{7,24},{8,23},{9,2... | collective-permute-start | bytes 307208 | tf_op jit(solution)/shard_map/ppermute | solution.py:55
  31.3 0.4 shard_map.145
  31.7 0.1 collective-permute-start.11
  31.8 3.8 %collective-permute-start.12 = (bf16[400,128]{1,0:T(8,128)(2,1)S(1)}, bf16[400,128]{1,0:T(8,128)(2,1)S(1)}, u32[]{:S(2)}, u32[]{:S(2)}) collective-permute-start(bf16[400,128]{1,0:T(8,128)(2,1)S(1)} %get-tuple-element.86), channel_id=1, source_target_pairs={{0,25},{1,24},{2,11},{3,10},{4,29},{5,28},{6,15},{7,14},{8,17},{9,... | collective-permute-start | bytes 307208 | tf_op jit(solution)/shard_map/ppermute | solution.py:55
  35.6 0.0 collective-permute-done.8.refs_0_
  35.6 0.0 collective-permute-start.13
  35.6 0.0 collective-permute-done.9.refs_1_
  35.6 2.2 %collective-permute-start.14 = (bf16[400,128]{1,0:T(8,128)(2,1)S(1)}, bf16[400,128]{1,0:T(8,128)(2,1)S(1)}, u32[]{:S(2)}, u32[]{:S(2)}) collective-permute-start(bf16[400,128]{1,0:T(8,128)(2,1)S(1)} %get-tuple-element.88), channel_id=1, source_target_pairs={{0,7},{1,2},{2,1},{3,4},{4,3},{5,6},{6,5},{7,0},{8,15},{9,10},{10,... | collective-permute-start | bytes 307208 | tf_op jit(solution)/shard_map/ppermute | solution.py:55
  37.8 0.0 collective-permute-done.10.refs_2_
  37.8 0.2 collective-permute-start.15
  38.1 4.3 %shard_map.144 = (bf16[25,4,16,128]{3,2,1,0:T(8,128)(2,1)}, f32[25,8,8,128]{3,2,1,0:T(8,128)S(1)}, bf16[4,128,256]{2,1,0:T(8,128)(2,1)S(1)}) custom-call(bf16[1600,128]{1,0:T(8,128)(2,1)S(1)} %get-tuple-element.47.own_ref.refs_0_, bf16[1600,128]{1,0:T(8,128)(2,1)S(1)} %get-tuple-element.48.refs_1_, s32[1,256]{1,0:T(1,128)S(1)} %get-tuple-element.49.refs_2_, ...), custom_call_target="tpu_custom_call" | custom-call | tf_op jit(solution)/shard_map/pallas_call | solution.py:395
  42.4 0.0 collective-permute-done.11.refs_3_
  42.4 0.0 collective-permute-done.12.refs_4_
  42.4 0.5 %collective-permute-done.13.refs_5_ = bf16[400,128]{1,0:T(8,128)(2,1)S(1)} collective-permute-done((bf16[400,128]{1,0:T(8,128)(2,1)S(1)}, bf16[400,128]{1,0:T(8,128)(2,1)S(1)}, u32[]{:S(2)}, u32[]{:S(2)}) %collective-permute-start.13) | collective-permute-done | bytes 102432 | tf_op jit(solution)/shard_map/ppermute | solution.py:55
  42.9 0.0 collective-permute-done.14.refs_6_
  42.9 0.0 collective-permute-done.15.refs_7_
  42.9 1.2 %shard_map.146 = f32[25,64,128]{2,1,0:T(8,128)} custom-call(bf16[400,128]{1,0:T(8,128)(2,1)S(1)} %collective-permute-done.8.refs_0_, bf16[400,128]{1,0:T(8,128)(2,1)S(1)} %collective-permute-done.9.refs_1_, bf16[400,128]{1,0:T(8,128)(2,1)S(1)} %collective-permute-done.10.refs_2_, bf16[400,128]{1,0:T(8,128)(2,1)S(1)} %collective-permute-done.11.refs_3_, ...), custom_call_target="tpu_custom_call" | custom-call | tf_op jit(solution)/shard_map/pallas_call | solution.py:395
Async XLA Ops:
  2.0 11.0 %collective-permute-start = (bf16[400,128]{1,0:T(8,128)(2,1)S(1)}, bf16[400,128]{1,0:T(8,128)(2,1)S(1)}, u32[]{:S(2)}, u32[]{:S(2)}) collective-permute-start(bf16[400,128]{1,0:T(8,128)(2,1)S(1)} %get-tuple-element.53), channel_id=1, source_target_pairs={{0,8},{1,25},{2,10},{3,27},{4,12},{5,29},{6,14},{7,31},{8,0},{9,17... | collective-permute-start | bytes 307208 | tf_op jit(solution)/shard_map/ppermute | solution.py:55
  5.2 9.2 %collective-permute-start.1 = (bf16[400,128]{1,0:T(8,128)(2,1)S(1)}, bf16[400,128]{1,0:T(8,128)(2,1)S(1)}, u32[]{:S(2)}, u32[]{:S(2)}) collective-permute-start(bf16[400,128]{1,0:T(8,128)(2,1)S(1)} %get-tuple-element.54), channel_id=1, source_target_pairs={{0,24},{1,9},{2,26},{3,11},{4,28},{5,13},{6,30},{7,15},{8,16},{9,1... | collective-permute-start | bytes 307208 | tf_op jit(solution)/shard_map/ppermute | solution.py:55
  7.6 8.8 %collective-permute-start.2 = (bf16[400,128]{1,0:T(8,128)(2,1)S(1)}, bf16[400,128]{1,0:T(8,128)(2,1)S(1)}, u32[]{:S(2)}, u32[]{:S(2)}) collective-permute-start(bf16[400,128]{1,0:T(8,128)(2,1)S(1)} %get-tuple-element.55), channel_id=1, source_target_pairs={{0,31},{1,10},{2,9},{3,28},{4,27},{5,14},{6,13},{7,24},{8,23},{9,2... | collective-permute-start | bytes 307208 | tf_op jit(solution)/shard_map/ppermute | solution.py:55
  8.8 11.3 %collective-permute-start.3 = (bf16[400,128]{1,0:T(8,128)(2,1)S(1)}, bf16[400,128]{1,0:T(8,128)(2,1)S(1)}, u32[]{:S(2)}, u32[]{:S(2)}) collective-permute-start(bf16[400,128]{1,0:T(8,128)(2,1)S(1)} %get-tuple-element.56), channel_id=1, source_target_pairs={{0,15},{1,26},{2,25},{3,12},{4,11},{5,30},{6,29},{7,8},{8,7},{9,18... | collective-permute-start | bytes 307208 | tf_op jit(solution)/shard_map/ppermute | solution.py:55
  10.4 9.7 %collective-permute-start.4 = (bf16[400,128]{1,0:T(8,128)(2,1)S(1)}, bf16[400,128]{1,0:T(8,128)(2,1)S(1)}, u32[]{:S(2)}, u32[]{:S(2)}) collective-permute-start(bf16[400,128]{1,0:T(8,128)(2,1)S(1)} %get-tuple-element.57), channel_id=1, source_target_pairs={{0,25},{1,24},{2,11},{3,10},{4,29},{5,28},{6,15},{7,14},{8,17},{9,... | collective-permute-start | bytes 307208 | tf_op jit(solution)/shard_map/ppermute | solution.py:55
  13.1 7.3 %collective-permute-start.5 = (bf16[400,128]{1,0:T(8,128)(2,1)S(1)}, bf16[400,128]{1,0:T(8,128)(2,1)S(1)}, u32[]{:S(2)}, u32[]{:S(2)}) collective-permute-start(bf16[400,128]{1,0:T(8,128)(2,1)S(1)} %get-tuple-element.58), channel_id=1, source_target_pairs={{0,9},{1,8},{2,27},{3,26},{4,13},{5,12},{6,31},{7,30},{8,1},{9,0},... | collective-permute-start | bytes 307208 | tf_op jit(solution)/shard_map/ppermute | solution.py:55
  14.3 6.2 %collective-permute-start.6 = (bf16[400,128]{1,0:T(8,128)(2,1)S(1)}, bf16[400,128]{1,0:T(8,128)(2,1)S(1)}, u32[]{:S(2)}, u32[]{:S(2)}) collective-permute-start(bf16[400,128]{1,0:T(8,128)(2,1)S(1)} %get-tuple-element.59), channel_id=1, source_target_pairs={{0,7},{1,2},{2,1},{3,4},{4,3},{5,6},{6,5},{7,0},{8,15},{9,10},{10,... | collective-permute-start | bytes 307208 | tf_op jit(solution)/shard_map/ppermute | solution.py:55
  16.4 4.2 %collective-permute-start.7 = (bf16[400,128]{1,0:T(8,128)(2,1)S(1)}, bf16[400,128]{1,0:T(8,128)(2,1)S(1)}, u32[]{:S(2)}, u32[]{:S(2)}) collective-permute-start(bf16[400,128]{1,0:T(8,128)(2,1)S(1)} %get-tuple-element.60), channel_id=1, source_target_pairs={{0,1},{1,0},{2,3},{3,2},{4,5},{5,4},{6,7},{7,6},{8,9},{9,8},{10,11... | collective-permute-start | bytes 307208 | tf_op jit(solution)/shard_map/ppermute | solution.py:55
  24.3 11.4 %collective-permute-start.8 = (bf16[400,128]{1,0:T(8,128)(2,1)S(1)}, bf16[400,128]{1,0:T(8,128)(2,1)S(1)}, u32[]{:S(2)}, u32[]{:S(2)}) collective-permute-start(bf16[400,128]{1,0:T(8,128)(2,1)S(1)} %get-tuple-element.82), channel_id=1, source_target_pairs={{0,8},{1,25},{2,10},{3,27},{4,12},{5,29},{6,14},{7,31},{8,0},{9,17... | collective-permute-start | bytes 307208 | tf_op jit(solution)/shard_map/ppermute | solution.py:55
  26.1 9.5 %collective-permute-start.9 = (bf16[400,128]{1,0:T(8,128)(2,1)S(1)}, bf16[400,128]{1,0:T(8,128)(2,1)S(1)}, u32[]{:S(2)}, u32[]{:S(2)}) collective-permute-start(bf16[400,128]{1,0:T(8,128)(2,1)S(1)} %get-tuple-element.83), channel_id=1, source_target_pairs={{0,24},{1,9},{2,26},{3,11},{4,28},{5,13},{6,30},{7,15},{8,16},{9,1... | collective-permute-start | bytes 307208 | tf_op jit(solution)/shard_map/ppermute | solution.py:55
  27.7 10.2 %collective-permute-start.10 = (bf16[400,128]{1,0:T(8,128)(2,1)S(1)}, bf16[400,128]{1,0:T(8,128)(2,1)S(1)}, u32[]{:S(2)}, u32[]{:S(2)}) collective-permute-start(bf16[400,128]{1,0:T(8,128)(2,1)S(1)} %get-tuple-element.84), channel_id=1, source_target_pairs={{0,31},{1,10},{2,9},{3,28},{4,27},{5,14},{6,13},{7,24},{8,23},{9,2... | collective-permute-start | bytes 307208 | tf_op jit(solution)/shard_map/ppermute | solution.py:55
  31.7 10.7 %collective-permute-start.11 = (bf16[400,128]{1,0:T(8,128)(2,1)S(1)}, bf16[400,128]{1,0:T(8,128)(2,1)S(1)}, u32[]{:S(2)}, u32[]{:S(2)}) collective-permute-start(bf16[400,128]{1,0:T(8,128)(2,1)S(1)} %get-tuple-element.85), channel_id=1, source_target_pairs={{0,15},{1,26},{2,25},{3,12},{4,11},{5,30},{6,29},{7,8},{8,7},{9,18... | collective-permute-start | bytes 307208 | tf_op jit(solution)/shard_map/ppermute | solution.py:55
  31.8 10.6 %collective-permute-start.12 = (bf16[400,128]{1,0:T(8,128)(2,1)S(1)}, bf16[400,128]{1,0:T(8,128)(2,1)S(1)}, u32[]{:S(2)}, u32[]{:S(2)}) collective-permute-start(bf16[400,128]{1,0:T(8,128)(2,1)S(1)} %get-tuple-element.86), channel_id=1, source_target_pairs={{0,25},{1,24},{2,11},{3,10},{4,29},{5,28},{6,15},{7,14},{8,17},{9,... | collective-permute-start | bytes 307208 | tf_op jit(solution)/shard_map/ppermute | solution.py:55
  35.6 7.2 %collective-permute-start.13 = (bf16[400,128]{1,0:T(8,128)(2,1)S(1)}, bf16[400,128]{1,0:T(8,128)(2,1)S(1)}, u32[]{:S(2)}, u32[]{:S(2)}) collective-permute-start(bf16[400,128]{1,0:T(8,128)(2,1)S(1)} %get-tuple-element.87), channel_id=1, source_target_pairs={{0,9},{1,8},{2,27},{3,26},{4,13},{5,12},{6,31},{7,30},{8,1},{9,0},... | collective-permute-start | bytes 307208 | tf_op jit(solution)/shard_map/ppermute | solution.py:55
  35.6 7.2 %collective-permute-start.14 = (bf16[400,128]{1,0:T(8,128)(2,1)S(1)}, bf16[400,128]{1,0:T(8,128)(2,1)S(1)}, u32[]{:S(2)}, u32[]{:S(2)}) collective-permute-start(bf16[400,128]{1,0:T(8,128)(2,1)S(1)} %get-tuple-element.88), channel_id=1, source_target_pairs={{0,7},{1,2},{2,1},{3,4},{4,3},{5,6},{6,5},{7,0},{8,15},{9,10},{10,... | collective-permute-start | bytes 307208 | tf_op jit(solution)/shard_map/ppermute | solution.py:55
  37.8 5.0 %collective-permute-start.15 = (bf16[400,128]{1,0:T(8,128)(2,1)S(1)}, bf16[400,128]{1,0:T(8,128)(2,1)S(1)}, u32[]{:S(2)}, u32[]{:S(2)}) collective-permute-start(bf16[400,128]{1,0:T(8,128)(2,1)S(1)} %get-tuple-element.89), channel_id=1, source_target_pairs={{0,1},{1,0},{2,3},{3,2},{4,5},{5,4},{6,7},{7,6},{8,9},{9,8},{10,11... | collective-permute-start | bytes 307208 | tf_op jit(solution)/shard_map/ppermute | solution.py:55
